TPU v7x, 32 devices: a whole 2x2x4 slice. The times are simulated.
32 devices in a mesh: row: 8 (over y, x, core), col: 4 (over z).
Axes of the slice: x: 2, y: 2, z: 4, core: 2. Of those that a mesh axis runs over, the one named last changes fastest.
Arguments:
- node_features: bfloat16 [8192, 128], P(('row', 'col')), may hold values from -6 to 6
- tile_values: bfloat16 [8, 4, 384, 128, 128], P('row', 'col'), may hold values from -0.078125 to 0.078125
- tile_rows: int32 [8, 4, 384], P('row', 'col'), may hold values from 0 to 7
- tile_cols: int32 [8, 4, 384], P('row', 'col'), may hold values from 0 to 15
- tile_count: int32 [8, 4], P('row', 'col'), may hold values from 48 to 384, as said below
- labels: int32 [8192], P(('row', 'col')), may hold values from 0 to 46
- train_mask: int32 [8192], P(('row', 'col')), may hold values from 0 to 1, as said below
- hidden_weight: bfloat16 [128, 256], replicated, may hold values from -0.5 to 0.5
- hidden_bias: float32 [256], replicated, may hold values from -3 to 3
- class_weight: bfloat16 [256, 47], replicated, may hold values from -3.59375 to 3.59375
- class_bias: float32 [47], replicated, may hold values from -4 to 4
Outputs:
- hidden: bfloat16 [8192, 256], P(('row', 'col'))
- logits: float32 [47, 8192], P(None, ('row', 'col'))
- mean_loss: float32 [], replicated
- hidden_weight_grad: float32 [128, 256], replicated
- hidden_bias_grad: float32 [256], replicated
- class_weight_grad: float32 [256, 47], replicated
- class_bias_grad: float32 [47], replicated
Inputs may be any that keep to these rules, and one draw needn't show every extreme that they name: Slots s >= tile_count of a block are not part of it; some block has all 384 slots live. `train_mask`: at least one node is a training node.
All inputs are finite; a program needn't handle non-finite values.
Results may differ from a plain program's by a relative error of at most 0.025.
Values may be sent and summed in bfloat16 or wider, within the bound.
No kernel may reach another device: no remote copies, remote signals or barrier semaphores. Data moves between devices by JAX's collectives and lax.ppermute only.
A program may use at most 128 MiB of HBM per device.

v0:
```python
import functools
import math

import jax
import jax.numpy as jnp
from jax import lax
from jax.experimental import pallas as pl
from jax.experimental.pallas import tpu as pltpu
from jax.sharding import PartitionSpec as P


TILE = 128
MASK_CODE = 128
MIB = 1024 * 1024
WIRE = jnp.bfloat16
f32 = jnp.float32
bf16 = jnp.bfloat16


VMEM = pl.BlockSpec(memory_space=pltpu.VMEM)
SMEM = pl.BlockSpec(memory_space=pltpu.SMEM)
HBM = pl.BlockSpec(memory_space=pltpu.HBM)


def params(limit):
    return pltpu.CompilerParams(vmem_limit_bytes=limit)


def cost(flops, moved, transcendentals=0):
    return pl.CostEstimate(flops=flops, bytes_accessed=moved, transcendentals=transcendentals)


def dot(a, b, dims=((1,), (0,))):
    return lax.dot_general(a, b, (dims, ((), ())), preferred_element_type=f32)


def halves(value):
    high = value.astype(bf16)
    return high, (value - high.astype(f32)).astype(bf16)


def collect_kernel(group, depth, tile_cols, ids, count, rows_hbm, cols_hbm, values, total, ring, rows, cols, sem, table_sem):
    slots = values.shape[0]
    groups = slots // group
    spare = total.shape[0] - 1
    tables = [
        pltpu.make_async_copy(source, target, table_sem.at[k])
        for k, (source, target) in enumerate(((rows_hbm, rows), (cols_hbm, cols)))
    ]
    for table in tables:
        table.start()

    def copy(index, slot):
        return pltpu.make_async_copy(
            values.at[pl.ds(index * group, group)], ring.at[slot], sem.at[slot]
        )

    live = count[0, 0]
    groups_live = (live + group - 1) // group
    for slot in range(depth):
        @pl.when(slot < groups_live)
        def _():
            copy(slot, slot).start()

    @pl.loop(0, spare // 4)
    def _(place):
        for k in range(4):
            total[place * 4 + k] = jnp.zeros((TILE, TILE), f32)

    for table in tables:
        table.wait()

    @pl.loop(0, groups_live)
    def _(index):
        slot = lax.rem(index, depth)
        copy(index, slot).wait()
        for k in range(group):
            item = index * group + k
            place = rows[0, item] * tile_cols + cols[0, item]
            place = jnp.where(item < live, place, spare)
            total[place] = total[place] + ring[slot, k].astype(f32)

        if depth < groups:
            @pl.when(index + depth < groups_live)
            def _():
                copy(index + depth, slot).start()


def collect(ids, values, rows, cols, count, tile_rows, tile_cols):
    slots = values.shape[0]
    n_places = tile_rows * tile_cols
    group = math.gcd(slots, 16)
    small = n_places <= 128
    depth = slots // group if small else min(slots // group, 8)
    rows, cols = (pltpu.with_memory_space_constraint(x, pltpu.HBM) for x in (rows, cols))
    return pl.pallas_call(
        functools.partial(collect_kernel, group, depth, tile_cols),
        out_shape=jax.ShapeDtypeStruct((n_places + 1, TILE, TILE), f32),
        in_specs=[SMEM, SMEM, HBM, HBM, HBM],
        out_specs=VMEM,
        scratch_shapes=[
            pltpu.VMEM((depth, group, TILE, TILE), bf16),
            pltpu.SMEM((1, slots), jnp.int32),
            pltpu.SMEM((1, slots), jnp.int32),
            pltpu.SemaphoreType.DMA((depth,)),
            pltpu.SemaphoreType.DMA((2,)),
        ],
        compiler_params=params((44 if small else 56) * MIB),
        cost_estimate=cost(slots * TILE * TILE, slots * TILE * TILE * 2),
        name="collect",
    )(ids, count, rows, cols, values)


def position(row, k, n_row):
    other = row ^ k
    return (other & 1) * (n_row // 2) + (other >> 1)


def place_of(row, k, n_row, nodes):
    return pl.ds(pl.multiple_of(position(row, k, n_row) * nodes, nodes), nodes)


def stack(row, start, pieces, stacked):
    nodes = pieces[0].shape[0]
    for k, piece in enumerate(pieces):
        place = pl.multiple_of(((row ^ (start + 2 * k)) >> 1) * nodes, nodes)
        stacked[pl.ds(place, nodes), :] = piece[...]


def parity_columns(parity, columns):
    return pl.ds(pl.multiple_of(parity * (columns // 2), columns // 2), columns // 2)


def round_kernel(n_row, total, dense):
    tile_rows = dense.shape[0] // TILE
    tile_cols = dense.shape[1] // TILE
    each = tile_cols // n_row

    @pl.loop(0, tile_rows)
    def _(tile_row):
        lines = pl.ds(pl.multiple_of(tile_row * TILE, TILE), TILE)
        for tile_col in range(tile_cols):
            target = position(tile_col // each, 0, n_row) * each + tile_col % each
            lanes = pl.ds(target * TILE, TILE)
            dense[lines, lanes] = total[tile_row * tile_cols + tile_col].astype(bf16)


def round_block(total, lines, columns, n_row):
    return pl.pallas_call(
        functools.partial(round_kernel, n_row),
        out_shape=jax.ShapeDtypeStruct((lines, columns), bf16),
        in_specs=[VMEM],
        out_specs=VMEM,
        compiler_params=params(lines * columns * 6 + 6 * MIB),
        cost_estimate=cost(lines * columns, lines * columns * 6),
        name="round_block",
    )(total)


def first_near_kernel(n_row, ids, dense, *refs):
    pieces = refs[: n_row // 2]
    part, stacked = refs[n_row // 2 :]
    row = ids[0]
    stack(row, 0, pieces, stacked)
    part[...] = dot(dense[:, parity_columns(row & 1, dense.shape[1])], stacked[...])


def first_near(ids, dense, pieces):
    nodes, width = pieces[0].shape
    n_row = 2 * len(pieces)
    return pl.pallas_call(
        functools.partial(first_near_kernel, n_row),
        out_shape=jax.ShapeDtypeStruct((dense.shape[0], width), f32),
        in_specs=[SMEM, VMEM] + [VMEM] * len(pieces),
        out_specs=VMEM,
        scratch_shapes=[pltpu.VMEM((len(pieces) * nodes, width), bf16)],
        compiler_params=params(dense.size * 2 + 6 * MIB),
        cost_estimate=cost(dense.size * width, dense.size),
        name="first_near",
    )(ids, dense, *pieces)


def first_far_kernel(n_row, n_col, ids, dense, part, *refs):
    pieces = refs[: n_row // 2]
    outs, stacked = refs[n_row // 2 : -1], refs[-1]
    nodes = pieces[0].shape[0]
    row, col = ids[0], ids[1]
    stack(row, 1, pieces, stacked)
    columns = parity_columns(1 - (row & 1), dense.shape[1])
    for k in range(n_col):
        lines = pl.ds(pl.multiple_of((col ^ k) * nodes, nodes), nodes)
        outs[k][...] = (part[lines, :] + dot(dense[lines, columns], stacked[...])).astype(bf16)


def first_far(ids, dense, part, pieces, n_col):
    nodes, width = pieces[0].shape
    n_row = 2 * len(pieces)
    return pl.pallas_call(
        functools.partial(first_far_kernel, n_row, n_col),
        out_shape=[jax.ShapeDtypeStruct((nodes, width), bf16)] * n_col,
        in_specs=[SMEM, VMEM, VMEM] + [VMEM] * len(pieces),
        out_specs=[VMEM] * n_col,
        scratch_shapes=[pltpu.VMEM((len(pieces) * nodes, width), bf16)],
        compiler_params=params(dense.size * 2 + 6 * MIB),
        cost_estimate=cost(dense.size * width, dense.size),
        name="first_far",
    )(ids, dense, part, *pieces)


def hidden_pieces(row, start, weight, bias, class_weight, pieces, column, stacked, own):
    nodes = pieces[0].shape[0]
    for k, piece in enumerate(pieces):
        other = start + 2 * k
        pre = dot(piece[...], weight[...]) + bias[...]
        hidden = (pre * (1.0 / (1.0 + jnp.exp(-pre)))).astype(bf16)
        place = pl.ds(pl.multiple_of(((row ^ other) >> 1) * nodes, nodes), nodes)
        column[place, :] = hidden
        if other == 0:
            own[...] = hidden
        high, low = halves(dot(hidden, class_weight[...], ((1,), (1,))))
        stacked[place, :] = jnp.concatenate([high, low], axis=1)


def both_halves(value):
    lanes = value.shape[1] // 2
    return value[:, :lanes] + value[:, lanes:]


def hidden_near_kernel(n_row, ids, dense, weight, bias, class_weight, *refs):
    pieces = refs[: n_row // 2]
    hidden_out, column, part, stacked = refs[n_row // 2 :]
    row = ids[0]
    hidden_pieces(row, 0, weight, bias, class_weight, pieces, column, stacked, hidden_out)
    part[...] = both_halves(dot(dense[:, parity_columns(row & 1, dense.shape[1])], stacked[...]))


def hidden_near(ids, dense, weight, bias, class_weight, pieces):
    nodes = pieces[0].shape[0]
    n_row = 2 * len(pieces)
    width = weight.shape[1]
    lanes = class_weight.shape[0]
    column = n_row * nodes
    return pl.pallas_call(
        functools.partial(hidden_near_kernel, n_row),
        out_shape=[
            jax.ShapeDtypeStruct((nodes, width), bf16),
            jax.ShapeDtypeStruct((column // 2, width), bf16),
            jax.ShapeDtypeStruct((dense.shape[0], lanes), f32),
        ],
        in_specs=[SMEM] + [VMEM] * (4 + len(pieces)),
        out_specs=[VMEM] * 3,
        scratch_shapes=[pltpu.VMEM((column // 2, 2 * lanes), bf16)],
        compiler_params=params(dense.size * 2 + column * width * 8 + 6 * MIB),
        cost_estimate=cost(2 * dense.size * lanes, dense.size, column * width),
        name="hidden_near",
    )(ids, dense, weight, bias, class_weight, *pieces)


def hidden_far_kernel(n_row, n_col, ids, dense, weight, bias, class_weight, code, part, near, *refs):
    pieces = refs[: n_row // 2]
    column, term_out, stacked = refs[n_row // 2 :]
    nodes = pieces[0].shape[0]
    row, col = ids[0], ids[1]
    half = near.shape[0]
    parity = row & 1
    column[pl.ds(pl.multiple_of(parity * half, half), half), :] = near[...]
    other = column.at[pl.ds(pl.multiple_of((1 - parity) * half, half), half), :]
    hidden_pieces(row, 1, weight, bias, class_weight, pieces, other, stacked, None)
    both = dot(dense[:, parity_columns(1 - (row & 1), dense.shape[1])], stacked[...])
    term = (part[...] + both_halves(both)).T[: term_out.shape[0]]
    slice_of = lax.broadcasted_iota(jnp.int32, term.shape, 1) // nodes
    line = lax.broadcasted_iota(jnp.int32, term.shape, 0)
    codes = jnp.where(slice_of == col, jnp.concatenate([code[...]] * n_col, axis=1), 0.0)
    term_out[...] = jnp.where(line == term.shape[0] - 1, codes, term).astype(bf16)


def hidden_far(ids, dense, weight, bias, class_weight, code, part, near, pieces, n_col, lines):
    nodes = pieces[0].shape[0]
    n_row = 2 * len(pieces)
    lanes = class_weight.shape[0]
    return pl.pallas_call(
        functools.partial(hidden_far_kernel, n_row, n_col),
        out_shape=[
            jax.ShapeDtypeStruct((2 * near.shape[0], near.shape[1]), bf16),
            jax.ShapeDtypeStruct((lines, n_col * nodes), bf16),
        ],
        in_specs=[SMEM] + [VMEM] * (7 + len(pieces)),
        out_specs=[VMEM] * 2,
        scratch_shapes=[pltpu.VMEM((near.shape[0], 2 * lanes), bf16)],
        compiler_params=params(dense.size * 2 + near.size * 16 + 6 * MIB),
        cost_estimate=cost(2 * dense.size * lanes, dense.size, 2 * near.size),
        name="hidden_far",
    )(ids, dense, weight, bias, class_weight, code, part, near, *pieces)


def slope_kernel(n_row, ids, weight, bias, *refs):
    pieces = refs[:n_row]
    slope_out, turned_out = refs[n_row:]
    nodes = pieces[0].shape[0]
    row = ids[0]
    for k in range(n_row):
        pre = dot(pieces[k][...], weight[...]) + bias[...]
        sigma = 1.0 / (1.0 + jnp.exp(-pre))
        place = place_of(row, k, n_row, nodes)
        slope_out[place, :] = sigma * (1.0 + pre * (1.0 - sigma))
        turned_out[:, place] = pieces[k][...].T


def slopes(ids, weight, bias, pieces):
    nodes, features = pieces[0].shape
    n_row = len(pieces)
    width = weight.shape[1]
    column = n_row * nodes
    return pl.pallas_call(
        functools.partial(slope_kernel, n_row),
        out_shape=[
            jax.ShapeDtypeStruct((column, width), f32),
            jax.ShapeDtypeStruct((features, column), bf16),
        ],
        in_specs=[SMEM] + [VMEM] * (2 + n_row),
        out_specs=[VMEM] * 2,
        compiler_params=params(column * width * 8 + 4 * MIB),
        cost_estimate=cost(2 * column * features * width, column * width * 4, column * width * 2),
        name="slopes",
    )(ids, weight, bias, *pieces)


def tree_sum(parts):
    parts = [part.astype(f32) for part in parts]
    while len(parts) > 1:
        parts = [parts[k] + parts[k + 1] for k in range(0, len(parts), 2)]
    return parts[0]


def gradient_kernel(n_col, classes, ids, dense, column, slope, turned, class_weight_turned, class_bias, *refs):
    terms = refs[:n_col]
    logits_out, keep_out, send_out, scratch, packed = refs[n_col:]
    lines, nodes_row = terms[0].shape
    nodes = nodes_row // n_col
    features = turned.shape[0]
    width = column.shape[1]
    row, col = ids[0], ids[1]
    total = tree_sum([term[...] for term in terms])
    code = total[lines - 1 :, :]
    live = (code >= MASK_CODE).astype(f32)
    label = (code - MASK_CODE * live).astype(jnp.int32)
    line = lax.broadcasted_iota(jnp.int32, total.shape, 0)
    bias = jnp.broadcast_to(class_bias[...], (8, class_bias.shape[1])).T[:lines, :1]
    logits = jnp.where(line < classes, total + bias, -jnp.inf)
    scratch[...] = logits
    own = pl.ds(pl.multiple_of(col * nodes, nodes), nodes)
    logits_out[...] = scratch[:classes, own]
    top = jnp.max(logits, axis=0, keepdims=True)
    log_total = top + jnp.log(jnp.sum(jnp.exp(logits - top), axis=0, keepdims=True))
    chosen = line == label
    picked = jnp.sum(jnp.where(chosen, logits, 0.0), axis=0, keepdims=True)
    grad = (jnp.exp(logits - log_total) - chosen.astype(f32)) * live
    high, low = halves(grad)
    stacked = jnp.concatenate([high, low], axis=0)
    both = dot(stacked, dense[...])
    back = both[:lines] + both[lines:]
    back_high, back_low = halves(back)
    back_both = jnp.concatenate([back_high, back_low], axis=0)
    class_both = dot(back_both, column[...])
    packed[pl.ds(features, lines), :] = class_both[:lines] + class_both[lines:]
    twice = jnp.concatenate([class_weight_turned[:lines, :]] * 2, axis=0)
    hidden_grad = dot(back_both, twice, ((0,), (0,)))
    pre_grad = hidden_grad * slope[...]
    packed[pl.ds(0, features), :] = dot(turned[...], pre_grad.astype(bf16))
    packed[pl.ds(features + lines - 1, 1), :] = jnp.sum(pre_grad, axis=0, keepdims=True)
    here = (lax.broadcasted_iota(jnp.int32, (8, nodes_row), 1) // nodes == col).astype(f32)
    ours = here.astype(bf16)
    class_sum = dot(ours, high, ((1,), (1,))) + dot(ours, low, ((1,), (1,)))
    class_sum = jnp.concatenate([class_sum, jnp.zeros((8, width - lines), f32)], axis=1)
    loss = jnp.sum((log_total - picked) * live * here[:1])
    members = jnp.sum(live * here[:1])
    lane = lax.broadcasted_iota(jnp.int32, (8, width), 1)
    entry = lax.broadcasted_iota(jnp.int32, (8, width), 0)
    loss = jnp.full((8, width), loss, f32)
    loss_high = loss.astype(bf16).astype(f32)
    loss_middle = (loss - loss_high).astype(bf16).astype(f32)
    loss_low = loss - loss_high - loss_middle
    values = jnp.where(entry == 0, loss_high, jnp.where(entry == 1, loss_middle, loss_low))
    values = jnp.where(entry == 3, members, jnp.where(entry < 3, values, 0.0))
    tail = jnp.where(lane == row * n_col + col, values, 0.0)
    packed[pl.ds(features + lines, 8), :] = class_sum
    packed[pl.ds(features + lines + 8, 8), :] = tail
    part = packed.shape[0] // 2
    core = row & 1
    keep_out[...] = packed[pl.ds(pl.multiple_of(core * part, 8), part), :].astype(keep_out.dtype)
    send_out[...] = packed[pl.ds(pl.multiple_of((1 - core) * part, 8), part), :].astype(send_out.dtype)


def gradients(ids, dense, column, slope, turned, class_weight_turned, class_bias, terms, classes):
    n_col = len(terms)
    lines, nodes_row = terms[0].shape
    width = column.shape[1]
    packed = turned.shape[0] + lines + 16
    return pl.pallas_call(
        functools.partial(gradient_kernel, n_col, classes),
        out_shape=[
            jax.ShapeDtypeStruct((classes, nodes_row // n_col), f32),
            jax.ShapeDtypeStruct((packed // 2, width), WIRE),
            jax.ShapeDtypeStruct((packed // 2, width), WIRE),
        ],
        in_specs=[SMEM] + [VMEM] * (6 + n_col),
        out_specs=[VMEM] * 3,
        scratch_shapes=[
            pltpu.VMEM((lines, nodes_row), f32),
            pltpu.VMEM((packed, width), f32),
        ],
        compiler_params=params(dense.size * 2 + column.size * 16 + 6 * MIB),
        cost_estimate=cost(4 * dense.size * lines, dense.size * 2),
        name="gradients",
    )(ids, dense, column, slope, turned, class_weight_turned, class_bias, *terms)


def finish_kernel(features, lines, classes, ids, mine, other, loss_out, weight_out, bias_out, class_out, class_bias_out, packed):
    part = mine.shape[0]
    core = ids[0] & 1
    packed[pl.ds(pl.multiple_of(core * part, 8), part), :] = mine[...].astype(f32)
    packed[pl.ds(pl.multiple_of((1 - core) * part, 8), part), :] = other[...].astype(f32)
    tail = packed[pl.ds(features + lines + 8, 8), :]
    sums = jnp.sum(tail, axis=1, keepdims=True)
    members = sums[3:4]
    loss_out[...] = (sums[0:1] + sums[1:2] + sums[2:3]) / members
    weight_out[...] = packed[pl.ds(0, features), :] / members
    bias_out[...] = packed[pl.ds(features + lines - 1, 1), :] / members
    class_out[...] = packed[pl.ds(features, classes), :] / members
    class_bias_out[...] = packed[pl.ds(features + lines, 1), :][:, :classes] / members


def finish(ids, mine, other, features, lines, classes):
    part, width = mine.shape
    return pl.pallas_call(
        functools.partial(finish_kernel, features, lines, classes),
        out_shape=[
            jax.ShapeDtypeStruct((1, 1), f32),
            jax.ShapeDtypeStruct((features, width), f32),
            jax.ShapeDtypeStruct((1, width), f32),
            jax.ShapeDtypeStruct((classes, width), f32),
            jax.ShapeDtypeStruct((1, classes), f32),
        ],
        in_specs=[SMEM, VMEM, VMEM],
        out_specs=[VMEM] * 5,
        scratch_shapes=[pltpu.VMEM((2 * part, width), f32)],
        compiler_params=params(4 * MIB),
        name="finish",
    )(ids, mine, other)


def swap(value, axis, mask):
    size = lax.axis_size(axis)
    return lax.ppermute(value, axis, [(k, k ^ mask) for k in range(size)])


def gather_row(value):
    size = lax.axis_size("row")
    even = [value] + [swap(value, "row", k) for k in range(2, size, 2)]
    odd = [swap(even[0], "row", 1)]
    odd += [swap(piece, "row", 1) for piece in even[1:]]
    return even, odd


def sum_over(value, axis, low, high):
    while low < high:
        step = min(2, high - low)
        parts = [value.astype(WIRE)]
        parts += [swap(parts[0], axis, k << low) for k in range(1, 1 << step)]
        value = tree_sum(parts)
        low += step
    return value


def step(
    node_features,
    tile_values,
    tile_rows,
    tile_cols,
    tile_count,
    labels,
    train_mask,
    hidden_weight,
    hidden_bias,
    class_weight,
    class_bias,
):
    nodes, features = node_features.shape
    classes = class_weight.shape[1]
    n_row, n_col = lax.axis_size("row"), lax.axis_size("col")
    row_bits, col_bits = n_row.bit_length() - 1, n_col.bit_length() - 1
    lines = (classes // 16 + 1) * 16
    ids = jnp.stack([lax.axis_index("row"), lax.axis_index("col")]).astype(jnp.int32)
    code = (labels + MASK_CODE * train_mask).astype(f32)[None, :]
    bias = hidden_bias[None, :]
    class_turned = jnp.pad(class_weight.T, ((0, TILE - classes), (0, 0)))
    class_bias_lanes = jnp.pad(class_bias, (0, TILE - classes))[None, :]

    near, far = gather_row(node_features)
    total = collect(
        ids, tile_values[0, 0], tile_rows[0], tile_cols[0], tile_count, n_col * nodes // TILE, n_row * nodes // TILE
    )
    dense = round_block(total, n_col * nodes, n_row * nodes, n_row)
    part = first_near(ids, dense, near)
    terms = first_far(ids, dense, part, far, n_col)
    arrived = [terms[0]] + [swap(terms[k], "col", k) for k in range(1, n_col)]
    first_agg = tree_sum(arrived).astype(bf16)
    near, far = gather_row(first_agg)
    pieces = [piece for pair in zip(near, far) for piece in pair]
    hidden, column_near, part = hidden_near(ids, dense, hidden_weight, bias, class_turned, near)
    column, term = hidden_far(
        ids, dense, hidden_weight, bias, class_turned, code, part, column_near, far, n_col, lines
    )
    class_terms = [term] + [swap(term, "col", k) for k in range(1, n_col)]
    slope, turned = slopes(ids, hidden_weight, bias, pieces)
    logits, keep, send = gradients(
        ids, dense, column, slope, turned, class_turned, class_bias_lanes, class_terms, classes
    )
    part = keep.astype(f32) + swap(send, "row", 1).astype(f32)
    part = sum_over(part, "row", 1, row_bits)
    part = sum_over(part, "col", 0, col_bits)
    mine = part.astype(WIRE)
    other = swap(mine, "row", 1)
    loss, weight_grad, bias_grad, class_grad, class_bias_grad = finish(
        ids, mine, other, features, lines, classes
    )
    return (
        hidden,
        logits,
        loss[0, 0],
        weight_grad,
        bias_grad[0],
        class_grad.T,
        class_bias_grad[0],
    )


def solution(mesh):
    in_specs = (
        P(("row", "col"), None),
        P("row", "col", None, None, None),
        P("row", "col", None),
        P("row", "col", None),
        P("row", "col"),
        P(("row", "col")),
        P(("row", "col")),
        P(),
        P(),
        P(),
        P(),
    )
    out_specs = (P(("row", "col"), None), P(None, ("row", "col")), P(), P(), P(), P(), P())
    return jax.shard_map(step, mesh=mesh, in_specs=in_specs, out_specs=out_specs, check_vma=False)
```

profile of v0, /device:TPU:0, one launch (start us, length us, event | category | flops | bytes accessed | tf_op | source)
XLA Modules:
  0.0 74.3 jit_solution(6506497450741394115)
XLA Ops:
  0.6 3.0 %collective-permute-start = (bf16[256,128]{1,0:T(8,128)(2,1)}, bf16[256,128]{1,0:T(8,128)(2,1)S(1)}, u32[]{:S(2)}, u32[]{:S(2)}) collective-permute-start(bf16[256,128]{1,0:T(8,128)(2,1)} %refs_0_.1), channel_id=1, source_target_pairs={{0,8},{4,12},{8,0},{12,4},{16,24},{20,28},{24,16},{28,20},{1,9},{5... | collective-permute-start | bytes 196616 | tf_op jit(solution)/shard_map/ppermute | solution.py:454
  3.7 1.5 %collective-permute-start.1 = (bf16[256,128]{1,0:T(8,128)(2,1)}, bf16[256,128]{1,0:T(8,128)(2,1)S(1)}, u32[]{:S(2)}, u32[]{:S(2)}) collective-permute-start(bf16[256,128]{1,0:T(8,128)(2,1)} %refs_0_.1), channel_id=1, source_target_pairs={{0,16},{4,20},{8,24},{12,28},{16,0},{20,4},{24,8},{28,12},{1,17},{... | collective-permute-start | bytes 196616 | tf_op jit(solution)/shard_map/ppermute | solution.py:454
  5.2 0.0 collective-permute-start.2
  5.2 1.1 %collective-permute-done.refs_1_ = bf16[256,128]{1,0:T(8,128)(2,1)S(1)} collective-permute-done((bf16[256,128]{1,0:T(8,128)(2,1)}, bf16[256,128]{1,0:T(8,128)(2,1)S(1)}, u32[]{:S(2)}, u32[]{:S(2)}) %collective-permute-start) | collective-permute-done | bytes 65568 | tf_op jit(solution)/shard_map/ppermute | solution.py:454
  6.3 1.8 %collective-permute-done.1.refs_2_ = bf16[256,128]{1,0:T(8,128)(2,1)S(1)} collective-permute-done((bf16[256,128]{1,0:T(8,128)(2,1)}, bf16[256,128]{1,0:T(8,128)(2,1)S(1)}, u32[]{:S(2)}, u32[]{:S(2)}) %collective-permute-start.1) | collective-permute-done | bytes 65568 | tf_op jit(solution)/shard_map/ppermute | solution.py:454
  8.1 2.4 %collective-permute-done.2.refs_3_ = bf16[256,128]{1,0:T(8,128)(2,1)S(1)} collective-permute-done((bf16[256,128]{1,0:T(8,128)(2,1)}, bf16[256,128]{1,0:T(8,128)(2,1)S(1)}, u32[]{:S(2)}, u32[]{:S(2)}) %collective-permute-start.2) | collective-permute-done | bytes 65568 | tf_op jit(solution)/shard_map/ppermute | solution.py:454
  10.6 0.1 pad_add_fusion.ids
  11.3 2.4 %collect.1.total = f32[129,128,128]{2,1,0:T(8,128)S(1)} custom-call(s32[2]{0:T(128)S(1)} %pad_add_fusion.ids, s32[1,1]{1,0:T(1,128)S(6)} %copy.18.count, s32[1,384]{1,0:T(1,128)} %bitcast.20, s32[1,384]{1,0:T(1,128)} %bitcast.21, bf16[384,128,128]{2,1,0:T(8,128)(2,1)} %bitcast.18), custom_call_target="tpu_custom_call" | custom-call | flops 6291456 | bytes 12582912 | tf_op jit(solution)/shard_map/collect/pallas_call | solution.py:96
  13.8 0.8 %round_block.1.dense = bf16[1024,2048]{1,0:T(8,128)(2,1)S(1)} custom-call(f32[129,128,128]{2,1,0:T(8,128)S(1)} %collect.1.total), custom_call_target="tpu_custom_call" | custom-call | flops 2097152 | bytes 12582912 | tf_op jit(solution)/shard_map/round_block/pallas_call | solution.py:149
  14.7 1.3 %first_near.1.part = f32[1024,128]{1,0:T(8,128)S(1)} custom-call(s32[2]{0:T(128)S(1)} %pad_add_fusion.ids, bf16[1024,2048]{1,0:T(8,128)(2,1)S(1)} %round_block.1.dense, bf16[256,128]{1,0:T(8,128)(2,1)S(1)} %copy-done.1, bf16[256,128]{1,0:T(8,128)(2,1)S(1)} %collective-permute-done.refs_1_, bf16[256,128]{1,0:T(8,128)(2,1)S(1)} %collective-permute-done.1.refs_2_, ...), custom_call_target="tpu_custom_call" | custom-call | flops 268435456 | bytes 2097152 | tf_op jit(solution)/shard_map/first_near/pallas_call | solution.py:171
  16.0 1.3 %first_far.1 = (bf16[256,128]{1,0:T(8,128)(2,1)S(1)}, bf16[256,128]{1,0:T(8,128)(2,1)S(1)}, bf16[256,128]{1,0:T(8,128)(2,1)S(1)}, bf16[256,128]{1,0:T(8,128)(2,1)S(1)}) custom-call(s32[2]{0:T(128)S(1)} %pad_add_fusion.ids, bf16[1024,2048]{1,0:T(8,128)(2,1)S(1)} %round_block.1.dense, f32[1024,128]{1,0:T(8,128)S(1)} %first_near.1.part, ...), custom_call_target="tpu_custom_call" | custom-call | flops 268435456 | bytes 2097152 | tf_op jit(solution)/shard_map/first_far/pallas_call | solution.py:198
  17.3 1.6 %collective-permute-start.7 = (bf16[256,128]{1,0:T(8,128)(2,1)S(1)}, bf16[256,128]{1,0:T(8,128)(2,1)S(1)}, u32[]{:S(2)}, u32[]{:S(2)}) collective-permute-start(bf16[256,128]{1,0:T(8,128)(2,1)S(1)} %get-tuple-element.27), channel_id=1, source_target_pairs={{0,1},{1,0},{2,3},{3,2},{4,5},{5,4},{6,7},{7,6},{8,9},{9,8},{10,11... | collective-permute-start | bytes 196616 | tf_op jit(solution)/shard_map/ppermute | solution.py:454
  18.9 3.2 %collective-permute-start.8 = (bf16[256,128]{1,0:T(8,128)(2,1)S(1)}, bf16[256,128]{1,0:T(8,128)(2,1)S(1)}, u32[]{:S(2)}, u32[]{:S(2)}) collective-permute-start(bf16[256,128]{1,0:T(8,128)(2,1)S(1)} %get-tuple-element.28), channel_id=1, source_target_pairs={{0,2},{1,3},{2,0},{3,1},{4,6},{5,7},{6,4},{7,5},{8,10},{9,11},{10,... | collective-permute-start | bytes 196616 | tf_op jit(solution)/shard_map/ppermute | solution.py:454
  22.1 0.0 collective-permute-start.9
  22.2 4.3 %collective-permute-done.8 = bf16[256,128]{1,0:T(8,128)(2,1)S(1)} collective-permute-done((bf16[256,128]{1,0:T(8,128)(2,1)S(1)}, bf16[256,128]{1,0:T(8,128)(2,1)S(1)}, u32[]{:S(2)}, u32[]{:S(2)}) %collective-permute-start.8) | collective-permute-done | bytes 65568 | tf_op jit(solution)/shard_map/ppermute | solution.py:454
  26.5 1.8 %collective-permute-done.9 = bf16[256,128]{1,0:T(8,128)(2,1)S(1)} collective-permute-done((bf16[256,128]{1,0:T(8,128)(2,1)S(1)}, bf16[256,128]{1,0:T(8,128)(2,1)S(1)}, u32[]{:S(2)}, u32[]{:S(2)}) %collective-permute-start.9) | collective-permute-done | bytes 65568 | tf_op jit(solution)/shard_map/ppermute | solution.py:454
  28.3 0.9 %collective-permute-start.10 = (bf16[256,128]{1,0:T(8,128)(2,1)S(1)}, bf16[256,128]{1,0:T(8,128)(2,1)S(1)}, u32[]{:S(2)}, u32[]{:S(2)}) collective-permute-start(bf16[256,128]{1,0:T(8,128)(2,1)S(1)} %add_convert_fusion.refs_0_), channel_id=1, source_target_pairs={{0,8},{4,12},{8,0},{12,4},{16,24},{20,28},{24,16},{28,20},{1,9},{5... | collective-permute-start | bytes 196616 | tf_op jit(solution)/shard_map/ppermute | solution.py:454
  29.2 0.4 collective-permute-start.11
  29.6 2.3 %collective-permute-start.12 = (bf16[256,128]{1,0:T(8,128)(2,1)S(1)}, bf16[256,128]{1,0:T(8,128)(2,1)S(1)}, u32[]{:S(2)}, u32[]{:S(2)}) collective-permute-start(bf16[256,128]{1,0:T(8,128)(2,1)S(1)} %add_convert_fusion.refs_0_), channel_id=1, source_target_pairs={{0,24},{4,28},{8,16},{12,20},{16,8},{20,12},{24,0},{28,4},{1,25},{... | collective-permute-start | bytes 196616 | tf_op jit(solution)/shard_map/ppermute | solution.py:454
  31.9 1.3 %collective-permute-done.10.refs_1_.refs_2_ = bf16[256,128]{1,0:T(8,128)(2,1)S(1)} collective-permute-done((bf16[256,128]{1,0:T(8,128)(2,1)S(1)}, bf16[256,128]{1,0:T(8,128)(2,1)S(1)}, u32[]{:S(2)}, u32[]{:S(2)}) %collective-permute-start.10) | collective-permute-done | bytes 65568 | tf_op jit(solution)/shard_map/ppermute | solution.py:454
  33.2 1.7 %collective-permute-done.11.refs_2_.refs_4_ = bf16[256,128]{1,0:T(8,128)(2,1)S(1)} collective-permute-done((bf16[256,128]{1,0:T(8,128)(2,1)S(1)}, bf16[256,128]{1,0:T(8,128)(2,1)S(1)}, u32[]{:S(2)}, u32[]{:S(2)}) %collective-permute-start.11) | collective-permute-done | bytes 65568 | tf_op jit(solution)/shard_map/ppermute | solution.py:454
  34.9 0.5 collective-permute-start.16
  35.5 1.8 %hidden_near.1 = (bf16[256,256]{1,0:T(8,128)(2,1)}, bf16[1024,256]{1,0:T(8,128)(2,1)S(1)}, f32[1024,128]{1,0:T(8,128)S(1)}) custom-call(s32[2]{0:T(128)S(1)} %pad_add_fusion.ids, bf16[1024,2048]{1,0:T(8,128)(2,1)S(1)} %round_block.1.dense, bf16[128,256]{1,0:T(8,128)(2,1)S(1)} %copy-done, f32[1,256]{1,0:T(1,128)S(1)} %bitcast.15, ...), custom_call_target="tpu_custom_call" | custom-call | flops 536870912 | bytes 2097152 | tf_op jit(solution)/shard_map/hidden_near/pallas_call | solution.py:243
  37.3 2.0 %hidden_far.1 = (bf16[2048,256]{1,0:T(8,128)(2,1)S(1)}, bf16[48,1024]{1,0:T(8,128)(2,1)S(1)}) custom-call(s32[2]{0:T(128)S(1)} %pad_add_fusion.ids, bf16[1024,2048]{1,0:T(8,128)(2,1)S(1)} %round_block.1.dense, bf16[128,256]{1,0:T(8,128)(2,1)S(1)} %copy-done, f32[1,256]{1,0:T(1,128)S(1)} %bitcast.16, ...), custom_call_target="tpu_custom_call" | custom-call | flops 536870912 | bytes 2097152 | tf_op jit(solution)/shard_map/hidden_far/pallas_call | solution.py:281
  39.3 0.6 collective-permute-start.17
  39.9 1.9 %collective-permute-start.18 = (bf16[48,1024]{1,0:T(8,128)(2,1)S(1)}, bf16[48,1024]{1,0:T(8,128)(2,1)S(1)}, u32[]{:S(2)}, u32[]{:S(2)}) collective-permute-start(bf16[48,1024]{1,0:T(8,128)(2,1)S(1)} %get-tuple-element.36.refs_0_), channel_id=1, source_target_pairs={{0,2},{1,3},{2,0},{3,1},{4,6},{5,7},{6,4},{7,5},{8,10},{9,11},{10,... | collective-permute-start | bytes 294920 | tf_op jit(solution)/shard_map/ppermute | solution.py:454
  41.7 2.0 %collective-permute-start.19 = (bf16[48,1024]{1,0:T(8,128)(2,1)S(1)}, bf16[48,1024]{1,0:T(8,128)(2,1)S(1)}, u32[]{:S(2)}, u32[]{:S(2)}) collective-permute-start(bf16[48,1024]{1,0:T(8,128)(2,1)S(1)} %get-tuple-element.36.refs_0_), channel_id=1, source_target_pairs={{0,3},{1,2},{2,1},{3,0},{4,7},{5,6},{6,5},{7,4},{8,11},{9,10},{10,... | collective-permute-start | bytes 294920 | tf_op jit(solution)/shard_map/ppermute | solution.py:454
  43.8 1.5 %slopes.1 = (f32[2048,256]{1,0:T(8,128)S(1)}, bf16[128,2048]{1,0:T(8,128)(2,1)S(1)}) custom-call(s32[2]{0:T(128)S(1)} %pad_add_fusion.ids, bf16[128,256]{1,0:T(8,128)(2,1)S(1)} %copy-done, f32[1,256]{1,0:T(1,128)S(1)} %bitcast.17, bf16[256,128]{1,0:T(8,128)(2,1)S(1)} %add_convert_fusion.refs_0_, ...), custom_call_target="tpu_custom_call" | custom-call | flops 134217728 | bytes 2097152 | tf_op jit(solution)/shard_map/slopes/pallas_call | solution.py:314
  45.3 0.5 collective-permute-done.17.refs_1_
  45.8 4.7 %collective-permute-done.18.refs_2_ = bf16[48,1024]{1,0:T(8,128)(2,1)S(1)} collective-permute-done((bf16[48,1024]{1,0:T(8,128)(2,1)S(1)}, bf16[48,1024]{1,0:T(8,128)(2,1)S(1)}, u32[]{:S(2)}, u32[]{:S(2)}) %collective-permute-start.18) | collective-permute-done | bytes 98336 | tf_op jit(solution)/shard_map/ppermute | solution.py:454
  50.5 2.4 %gradients.1 = (f32[47,256]{1,0:T(8,128)}, bf16[96,256]{1,0:T(8,128)(2,1)S(1)}, bf16[96,256]{1,0:T(8,128)(2,1)S(1)}) custom-call(s32[2]{0:T(128)S(1)} %pad_add_fusion.ids, bf16[1024,2048]{1,0:T(8,128)(2,1)S(1)} %round_block.1.dense, bf16[2048,256]{1,0:T(8,128)(2,1)S(1)} %get-tuple-element.33.column, f32[2048,256]{1,0:T(8,128)S(1)} %get-tuple-element.34.slope, ...), custom_call_target="tpu_custom_call" | custom-call | flops 402653184 | bytes 4194304 | tf_op jit(solution)/shard_map/gradients/pallas_call | solution.py:399
  53.0 0.1 collective-permute-start.20
  53.1 1.2 %collective-permute-done.20 = bf16[96,256]{1,0:T(8,128)(2,1)S(1)} collective-permute-done((bf16[96,256]{1,0:T(8,128)(2,1)S(1)}, bf16[96,256]{1,0:T(8,128)(2,1)S(1)}, u32[]{:S(2)}, u32[]{:S(2)}) %collective-permute-start.20) | collective-permute-done | bytes 49184 | tf_op jit(solution)/shard_map/ppermute | solution.py:454
  54.3 2.1 %collective-permute-start.21 = (bf16[96,256]{1,0:T(8,128)(2,1)S(1)}, bf16[96,256]{1,0:T(8,128)(2,1)S(1)}, u32[]{:S(2)}, u32[]{:S(2)}) collective-permute-start(bf16[96,256]{1,0:T(8,128)(2,1)S(1)} %add_convert_fusion.3), channel_id=1, source_target_pairs={{0,8},{4,12},{8,0},{12,4},{16,24},{20,28},{24,16},{28,20},{1,9},{5... | collective-permute-start | bytes 147464 | tf_op jit(solution)/shard_map/ppermute | solution.py:454
  56.4 1.3 %collective-permute-start.22 = (bf16[96,256]{1,0:T(8,128)(2,1)S(1)}, bf16[96,256]{1,0:T(8,128)(2,1)S(1)}, u32[]{:S(2)}, u32[]{:S(2)}) collective-permute-start(bf16[96,256]{1,0:T(8,128)(2,1)S(1)} %add_convert_fusion.3), channel_id=1, source_target_pairs={{0,16},{4,20},{8,24},{12,28},{16,0},{20,4},{24,8},{28,12},{1,17},{... | collective-permute-start | bytes 147464 | tf_op jit(solution)/shard_map/ppermute | solution.py:454
  57.7 0.3 collective-permute-start.23
  57.9 0.5 collective-permute-done.21
  58.5 2.0 %collective-permute-done.22 = bf16[96,256]{1,0:T(8,128)(2,1)S(1)} collective-permute-done((bf16[96,256]{1,0:T(8,128)(2,1)S(1)}, bf16[96,256]{1,0:T(8,128)(2,1)S(1)}, u32[]{:S(2)}, u32[]{:S(2)}) %collective-permute-start.22) | collective-permute-done | bytes 49184 | tf_op jit(solution)/shard_map/ppermute | solution.py:454
  60.5 2.2 %collective-permute-done.23 = bf16[96,256]{1,0:T(8,128)(2,1)S(1)} collective-permute-done((bf16[96,256]{1,0:T(8,128)(2,1)S(1)}, bf16[96,256]{1,0:T(8,128)(2,1)S(1)}, u32[]{:S(2)}, u32[]{:S(2)}) %collective-permute-start.23) | collective-permute-done | bytes 49184 | tf_op jit(solution)/shard_map/ppermute | solution.py:454
  62.7 2.0 %collective-permute-start.24 = (bf16[96,256]{1,0:T(8,128)(2,1)S(1)}, bf16[96,256]{1,0:T(8,128)(2,1)S(1)}, u32[]{:S(2)}, u32[]{:S(2)}) collective-permute-start(bf16[96,256]{1,0:T(8,128)(2,1)S(1)} %add_convert_fusion.2), channel_id=1, source_target_pairs={{0,1},{1,0},{2,3},{3,2},{4,5},{5,4},{6,7},{7,6},{8,9},{9,8},{10,11... | collective-permute-start | bytes 147464 | tf_op jit(solution)/shard_map/ppermute | solution.py:454
  64.7 1.0 %collective-permute-start.25 = (bf16[96,256]{1,0:T(8,128)(2,1)S(1)}, bf16[96,256]{1,0:T(8,128)(2,1)S(1)}, u32[]{:S(2)}, u32[]{:S(2)}) collective-permute-start(bf16[96,256]{1,0:T(8,128)(2,1)S(1)} %add_convert_fusion.2), channel_id=1, source_target_pairs={{0,2},{1,3},{2,0},{3,1},{4,6},{5,7},{6,4},{7,5},{8,10},{9,11},{10,... | collective-permute-start | bytes 147464 | tf_op jit(solution)/shard_map/ppermute | solution.py:454
  65.7 1.4 %collective-permute-start.26 = (bf16[96,256]{1,0:T(8,128)(2,1)S(1)}, bf16[96,256]{1,0:T(8,128)(2,1)S(1)}, u32[]{:S(2)}, u32[]{:S(2)}) collective-permute-start(bf16[96,256]{1,0:T(8,128)(2,1)S(1)} %add_convert_fusion.2), channel_id=1, source_target_pairs={{0,3},{1,2},{2,1},{3,0},{4,7},{5,6},{6,5},{7,4},{8,11},{9,10},{10,... | collective-permute-start | bytes 147464 | tf_op jit(solution)/shard_map/ppermute | solution.py:454
  67.1 0.1 collective-permute-done.24
  67.2 2.9 %collective-permute-done.25 = bf16[96,256]{1,0:T(8,128)(2,1)S(1)} collective-permute-done((bf16[96,256]{1,0:T(8,128)(2,1)S(1)}, bf16[96,256]{1,0:T(8,128)(2,1)S(1)}, u32[]{:S(2)}, u32[]{:S(2)}) %collective-permute-start.25) | collective-permute-done | bytes 49184 | tf_op jit(solution)/shard_map/ppermute | solution.py:454
  70.2 1.5 %collective-permute-done.26 = bf16[96,256]{1,0:T(8,128)(2,1)S(1)} collective-permute-done((bf16[96,256]{1,0:T(8,128)(2,1)S(1)}, bf16[96,256]{1,0:T(8,128)(2,1)S(1)}, u32[]{:S(2)}, u32[]{:S(2)}) %collective-permute-start.26) | collective-permute-done | bytes 49184 | tf_op jit(solution)/shard_map/ppermute | solution.py:454
  71.7 0.1 collective-permute-start.27
  71.8 1.2 %collective-permute-done.27.other = bf16[96,256]{1,0:T(8,128)(2,1)S(1)} collective-permute-done((bf16[96,256]{1,0:T(8,128)(2,1)S(1)}, bf16[96,256]{1,0:T(8,128)(2,1)S(1)}, u32[]{:S(2)}, u32[]{:S(2)}) %collective-permute-start.27) | collective-permute-done | bytes 49184 | tf_op jit(solution)/shard_map/ppermute | solution.py:454
  73.0 1.3 %finish.1 = (f32[1,1]{1,0:T(1,128)}, f32[128,256]{1,0:T(8,128)}, f32[1,256]{1,0:T(1,128)}, f32[47,256]{1,0:T(8,128)}, f32[1,47]{1,0:T(1,128)}) custom-call(s32[2]{0:T(128)S(1)} %pad_add_fusion.ids, bf16[96,256]{1,0:T(8,128)(2,1)S(1)} %add_convert_fusion.1.mine, bf16[96,256]{1,0:T(8,128)(2,1)S(1)} %collective-permute-done.27.other), custom_call_target="tpu_custom_call" | custom-call | tf_op jit(solution)/shard_map/finish/pallas_call | solution.py:435
  (39 shorter events, 0.2 us)
Async XLA Ops:
  0.6 5.7 %collective-permute-start = (bf16[256,128]{1,0:T(8,128)(2,1)}, bf16[256,128]{1,0:T(8,128)(2,1)S(1)}, u32[]{:S(2)}, u32[]{:S(2)}) collective-permute-start(bf16[256,128]{1,0:T(8,128)(2,1)} %refs_0_.1), channel_id=1, source_target_pairs={{0,8},{4,12},{8,0},{12,4},{16,24},{20,28},{24,16},{28,20},{1,9},{5... | collective-permute-start | bytes 196616 | tf_op jit(solution)/shard_map/ppermute | solution.py:454
  3.7 4.5 %collective-permute-start.1 = (bf16[256,128]{1,0:T(8,128)(2,1)}, bf16[256,128]{1,0:T(8,128)(2,1)S(1)}, u32[]{:S(2)}, u32[]{:S(2)}) collective-permute-start(bf16[256,128]{1,0:T(8,128)(2,1)} %refs_0_.1), channel_id=1, source_target_pairs={{0,16},{4,20},{8,24},{12,28},{16,0},{20,4},{24,8},{28,12},{1,17},{... | collective-permute-start | bytes 196616 | tf_op jit(solution)/shard_map/ppermute | solution.py:454
  5.2 5.4 %collective-permute-start.2 = (bf16[256,128]{1,0:T(8,128)(2,1)}, bf16[256,128]{1,0:T(8,128)(2,1)S(1)}, u32[]{:S(2)}, u32[]{:S(2)}) collective-permute-start(bf16[256,128]{1,0:T(8,128)(2,1)} %refs_0_.1), channel_id=1, source_target_pairs={{0,24},{4,28},{8,16},{12,20},{16,8},{20,12},{24,0},{28,4},{1,25},{... | collective-permute-start | bytes 196616 | tf_op jit(solution)/shard_map/ppermute | solution.py:454
  5.2 10.8 %collective-permute-start.3 = (bf16[256,128]{1,0:T(8,128)(2,1)}, bf16[256,128]{1,0:T(8,128)(2,1)S(1)}, u32[]{:S(2)}, u32[]{:S(2)}) collective-permute-start(bf16[256,128]{1,0:T(8,128)(2,1)} %refs_0_.1), channel_id=1, source_target_pairs={{0,4},{4,0},{8,12},{12,8},{16,20},{20,16},{24,28},{28,24},{1,5},{5... | collective-permute-start | bytes 196616 | tf_op jit(solution)/shard_map/ppermute | solution.py:454
  6.3 9.7 %collective-permute-start.4 = (bf16[256,128]{1,0:T(8,128)(2,1)S(1)}, bf16[256,128]{1,0:T(8,128)(2,1)S(1)}, u32[]{:S(2)}, u32[]{:S(2)}) collective-permute-start(bf16[256,128]{1,0:T(8,128)(2,1)S(1)} %collective-permute-done.refs_1_), channel_id=1, source_target_pairs={{0,4},{4,0},{8,12},{12,8},{16,20},{20,16},{24,28},{28,24},{1,5},{5... | collective-permute-start | bytes 196616 | tf_op jit(solution)/shard_map/ppermute | solution.py:454
  8.1 7.8 %collective-permute-start.5 = (bf16[256,128]{1,0:T(8,128)(2,1)S(1)}, bf16[256,128]{1,0:T(8,128)(2,1)S(1)}, u32[]{:S(2)}, u32[]{:S(2)}) collective-permute-start(bf16[256,128]{1,0:T(8,128)(2,1)S(1)} %collective-permute-done.1.refs_2_), channel_id=1, source_target_pairs={{0,4},{4,0},{8,12},{12,8},{16,20},{20,16},{24,28},{28,24},{1,5},{5... | collective-permute-start | bytes 196616 | tf_op jit(solution)/shard_map/ppermute | solution.py:454
  10.6 5.4 %collective-permute-start.6 = (bf16[256,128]{1,0:T(8,128)(2,1)S(1)}, bf16[256,128]{1,0:T(8,128)(2,1)S(1)}, u32[]{:S(2)}, u32[]{:S(2)}) collective-permute-start(bf16[256,128]{1,0:T(8,128)(2,1)S(1)} %collective-permute-done.2.refs_3_), channel_id=1, source_target_pairs={{0,4},{4,0},{8,12},{12,8},{16,20},{20,16},{24,28},{28,24},{1,5},{5... | collective-permute-start | bytes 196616 | tf_op jit(solution)/shard_map/ppermute | solution.py:454
  13.7 0.9 %copy-start.1 = (bf16[256,128]{1,0:T(8,128)(2,1)S(1)}, bf16[256,128]{1,0:T(8,128)(2,1)}, u32[]{:S(2)}) copy-start(bf16[256,128]{1,0:T(8,128)(2,1)} %refs_0_.1) | copy-start | bytes 196612
  13.8 21.7 %copy-start.4 = (s32[256]{0:T(256)S(1)}, s32[256]{0:T(256)}, u32[]{:S(2)}) copy-start(s32[256]{0:T(256)} %param.16) | copy-start | bytes 3076
  13.8 21.6 %copy-start.5 = (s32[256]{0:T(256)S(1)}, s32[256]{0:T(256)}, u32[]{:S(2)}) copy-start(s32[256]{0:T(256)} %param.17) | copy-start | bytes 3076
  13.8 21.6 %copy-start.3 = (bf16[256,47]{0,1:T(8,128)(2,1)S(1)}, bf16[256,47]{0,1:T(8,128)(2,1)}, u32[]{:S(2)}) copy-start(bf16[256,47]{0,1:T(8,128)(2,1)} %param.20) | copy-start | bytes 72196
  13.8 21.7 %copy-start = (bf16[128,256]{1,0:T(8,128)(2,1)S(1)}, bf16[128,256]{1,0:T(8,128)(2,1)}, u32[]{:S(2)}) copy-start(bf16[128,256]{1,0:T(8,128)(2,1)} %weight.5) | copy-start | bytes 196612
  13.8 21.6 %copy-start.2 = (f32[256]{0:T(256)S(1)}, f32[256]{0:T(256)}, u32[]{:S(2)}) copy-start(f32[256]{0:T(256)} %param.19) | copy-start | bytes 3076
  15.9 27.8 %copy-start.6 = (f32[47]{0:T(128)S(1)}, f32[47]{0:T(128)}, u32[]{:S(2)}) copy-start(f32[47]{0:T(128)} %param.21) | copy-start | bytes 568
  17.3 4.9 %collective-permute-start.7 = (bf16[256,128]{1,0:T(8,128)(2,1)S(1)}, bf16[256,128]{1,0:T(8,128)(2,1)S(1)}, u32[]{:S(2)}, u32[]{:S(2)}) collective-permute-start(bf16[256,128]{1,0:T(8,128)(2,1)S(1)} %get-tuple-element.27), channel_id=1, source_target_pairs={{0,1},{1,0},{2,3},{3,2},{4,5},{5,4},{6,7},{7,6},{8,9},{9,8},{10,11... | collective-permute-start | bytes 196616 | tf_op jit(solution)/shard_map/ppermute | solution.py:454
  18.9 7.6 %collective-permute-start.8 = (bf16[256,128]{1,0:T(8,128)(2,1)S(1)}, bf16[256,128]{1,0:T(8,128)(2,1)S(1)}, u32[]{:S(2)}, u32[]{:S(2)}) collective-permute-start(bf16[256,128]{1,0:T(8,128)(2,1)S(1)} %get-tuple-element.28), channel_id=1, source_target_pairs={{0,2},{1,3},{2,0},{3,1},{4,6},{5,7},{6,4},{7,5},{8,10},{9,11},{10,... | collective-permute-start | bytes 196616 | tf_op jit(solution)/shard_map/ppermute | solution.py:454
  22.1 6.2 %collective-permute-start.9 = (bf16[256,128]{1,0:T(8,128)(2,1)S(1)}, bf16[256,128]{1,0:T(8,128)(2,1)S(1)}, u32[]{:S(2)}, u32[]{:S(2)}) collective-permute-start(bf16[256,128]{1,0:T(8,128)(2,1)S(1)} %get-tuple-element.29), channel_id=1, source_target_pairs={{0,3},{1,2},{2,1},{3,0},{4,7},{5,6},{6,5},{7,4},{8,11},{9,10},{10,... | collective-permute-start | bytes 196616 | tf_op jit(solution)/shard_map/ppermute | solution.py:454
  28.3 4.9 %collective-permute-start.10 = (bf16[256,128]{1,0:T(8,128)(2,1)S(1)}, bf16[256,128]{1,0:T(8,128)(2,1)S(1)}, u32[]{:S(2)}, u32[]{:S(2)}) collective-permute-start(bf16[256,128]{1,0:T(8,128)(2,1)S(1)} %add_convert_fusion.refs_0_), channel_id=1, source_target_pairs={{0,8},{4,12},{8,0},{12,4},{16,24},{20,28},{24,16},{28,20},{1,9},{5... | collective-permute-start | bytes 196616 | tf_op jit(solution)/shard_map/ppermute | solution.py:454
  29.2 5.7 %collective-permute-start.11 = (bf16[256,128]{1,0:T(8,128)(2,1)S(1)}, bf16[256,128]{1,0:T(8,128)(2,1)S(1)}, u32[]{:S(2)}, u32[]{:S(2)}) collective-permute-start(bf16[256,128]{1,0:T(8,128)(2,1)S(1)} %add_convert_fusion.refs_0_), channel_id=1, source_target_pairs={{0,16},{4,20},{8,24},{12,28},{16,0},{20,4},{24,8},{28,12},{1,17},{... | collective-permute-start | bytes 196616 | tf_op jit(solution)/shard_map/ppermute | solution.py:454
  29.6 5.3 %collective-permute-start.12 = (bf16[256,128]{1,0:T(8,128)(2,1)S(1)}, bf16[256,128]{1,0:T(8,128)(2,1)S(1)}, u32[]{:S(2)}, u32[]{:S(2)}) collective-permute-start(bf16[256,128]{1,0:T(8,128)(2,1)S(1)} %add_convert_fusion.refs_0_), channel_id=1, source_target_pairs={{0,24},{4,28},{8,16},{12,20},{16,8},{20,12},{24,0},{28,4},{1,25},{... | collective-permute-start | bytes 196616 | tf_op jit(solution)/shard_map/ppermute | solution.py:454
  31.9 5.4 %collective-permute-start.13 = (bf16[256,128]{1,0:T(8,128)(2,1)S(1)}, bf16[256,128]{1,0:T(8,128)(2,1)S(1)}, u32[]{:S(2)}, u32[]{:S(2)}) collective-permute-start(bf16[256,128]{1,0:T(8,128)(2,1)S(1)} %add_convert_fusion.refs_0_), channel_id=1, source_target_pairs={{0,4},{4,0},{8,12},{12,8},{16,20},{20,16},{24,28},{28,24},{1,5},{5... | collective-permute-start | bytes 196616 | tf_op jit(solution)/shard_map/ppermute | solution.py:454
  33.2 4.1 %collective-permute-start.14 = (bf16[256,128]{1,0:T(8,128)(2,1)S(1)}, bf16[256,128]{1,0:T(8,128)(2,1)S(1)}, u32[]{:S(2)}, u32[]{:S(2)}) collective-permute-start(bf16[256,128]{1,0:T(8,128)(2,1)S(1)} %collective-permute-done.10.refs_1_.refs_2_), channel_id=1, source_target_pairs={{0,4},{4,0},{8,12},{12,8},{16,20},{20,16},{24,28},{28,24},{1,5},{5... | collective-permute-start | bytes 196616 | tf_op jit(solution)/shard_map/ppermute | solution.py:454
  34.9 2.4 %collective-permute-start.15 = (bf16[256,128]{1,0:T(8,128)(2,1)S(1)}, bf16[256,128]{1,0:T(8,128)(2,1)S(1)}, u32[]{:S(2)}, u32[]{:S(2)}) collective-permute-start(bf16[256,128]{1,0:T(8,128)(2,1)S(1)} %collective-permute-done.11.refs_2_.refs_4_), channel_id=1, source_target_pairs={{0,4},{4,0},{8,12},{12,8},{16,20},{20,16},{24,28},{28,24},{1,5},{5... | collective-permute-start | bytes 196616 | tf_op jit(solution)/shard_map/ppermute | solution.py:454
  34.9 2.5 %collective-permute-start.16 = (bf16[256,128]{1,0:T(8,128)(2,1)S(1)}, bf16[256,128]{1,0:T(8,128)(2,1)S(1)}, u32[]{:S(2)}, u32[]{:S(2)}) collective-permute-start(bf16[256,128]{1,0:T(8,128)(2,1)S(1)} %collective-permute-done.12.refs_3_.refs_6_), channel_id=1, source_target_pairs={{0,4},{4,0},{8,12},{12,8},{16,20},{20,16},{24,28},{28,24},{1,5},{5... | collective-permute-start | bytes 196616 | tf_op jit(solution)/shard_map/ppermute | solution.py:454
  39.3 6.5 %collective-permute-start.17 = (bf16[48,1024]{1,0:T(8,128)(2,1)S(1)}, bf16[48,1024]{1,0:T(8,128)(2,1)S(1)}, u32[]{:S(2)}, u32[]{:S(2)}) collective-permute-start(bf16[48,1024]{1,0:T(8,128)(2,1)S(1)} %get-tuple-element.36.refs_0_), channel_id=1, source_target_pairs={{0,1},{1,0},{2,3},{3,2},{4,5},{5,4},{6,7},{7,6},{8,9},{9,8},{10,11... | collective-permute-start | bytes 294920 | tf_op jit(solution)/shard_map/ppermute | solution.py:454
  39.9 10.7 %collective-permute-start.18 = (bf16[48,1024]{1,0:T(8,128)(2,1)S(1)}, bf16[48,1024]{1,0:T(8,128)(2,1)S(1)}, u32[]{:S(2)}, u32[]{:S(2)}) collective-permute-start(bf16[48,1024]{1,0:T(8,128)(2,1)S(1)} %get-tuple-element.36.refs_0_), channel_id=1, source_target_pairs={{0,2},{1,3},{2,0},{3,1},{4,6},{5,7},{6,4},{7,5},{8,10},{9,11},{10,... | collective-permute-start | bytes 294920 | tf_op jit(solution)/shard_map/ppermute | solution.py:454
  41.7 8.8 %collective-permute-start.19 = (bf16[48,1024]{1,0:T(8,128)(2,1)S(1)}, bf16[48,1024]{1,0:T(8,128)(2,1)S(1)}, u32[]{:S(2)}, u32[]{:S(2)}) collective-permute-start(bf16[48,1024]{1,0:T(8,128)(2,1)S(1)} %get-tuple-element.36.refs_0_), channel_id=1, source_target_pairs={{0,3},{1,2},{2,1},{3,0},{4,7},{5,6},{6,5},{7,4},{8,11},{9,10},{10,... | collective-permute-start | bytes 294920 | tf_op jit(solution)/shard_map/ppermute | solution.py:454
  53.0 1.3 %collective-permute-start.20 = (bf16[96,256]{1,0:T(8,128)(2,1)S(1)}, bf16[96,256]{1,0:T(8,128)(2,1)S(1)}, u32[]{:S(2)}, u32[]{:S(2)}) collective-permute-start(bf16[96,256]{1,0:T(8,128)(2,1)S(1)} %get-tuple-element.39), channel_id=1, source_target_pairs={{0,4},{4,0},{8,12},{12,8},{16,20},{20,16},{24,28},{28,24},{1,5},{5... | collective-permute-start | bytes 147464 | tf_op jit(solution)/shard_map/ppermute | solution.py:454
  54.3 4.2 %collective-permute-start.21 = (bf16[96,256]{1,0:T(8,128)(2,1)S(1)}, bf16[96,256]{1,0:T(8,128)(2,1)S(1)}, u32[]{:S(2)}, u32[]{:S(2)}) collective-permute-start(bf16[96,256]{1,0:T(8,128)(2,1)S(1)} %add_convert_fusion.3), channel_id=1, source_target_pairs={{0,8},{4,12},{8,0},{12,4},{16,24},{20,28},{24,16},{28,20},{1,9},{5... | collective-permute-start | bytes 147464 | tf_op jit(solution)/shard_map/ppermute | solution.py:454
  56.4 4.1 %collective-permute-start.22 = (bf16[96,256]{1,0:T(8,128)(2,1)S(1)}, bf16[96,256]{1,0:T(8,128)(2,1)S(1)}, u32[]{:S(2)}, u32[]{:S(2)}) collective-permute-start(bf16[96,256]{1,0:T(8,128)(2,1)S(1)} %add_convert_fusion.3), channel_id=1, source_target_pairs={{0,16},{4,20},{8,24},{12,28},{16,0},{20,4},{24,8},{28,12},{1,17},{... | collective-permute-start | bytes 147464 | tf_op jit(solution)/shard_map/ppermute | solution.py:454
  57.7 5.0 %collective-permute-start.23 = (bf16[96,256]{1,0:T(8,128)(2,1)S(1)}, bf16[96,256]{1,0:T(8,128)(2,1)S(1)}, u32[]{:S(2)}, u32[]{:S(2)}) collective-permute-start(bf16[96,256]{1,0:T(8,128)(2,1)S(1)} %add_convert_fusion.3), channel_id=1, source_target_pairs={{0,24},{4,28},{8,16},{12,20},{16,8},{20,12},{24,0},{28,4},{1,25},{... | collective-permute-start | bytes 147464 | tf_op jit(solution)/shard_map/ppermute | solution.py:454
  62.7 4.6 %collective-permute-start.24 = (bf16[96,256]{1,0:T(8,128)(2,1)S(1)}, bf16[96,256]{1,0:T(8,128)(2,1)S(1)}, u32[]{:S(2)}, u32[]{:S(2)}) collective-permute-start(bf16[96,256]{1,0:T(8,128)(2,1)S(1)} %add_convert_fusion.2), channel_id=1, source_target_pairs={{0,1},{1,0},{2,3},{3,2},{4,5},{5,4},{6,7},{7,6},{8,9},{9,8},{10,11... | collective-permute-start | bytes 147464 | tf_op jit(solution)/shard_map/ppermute | solution.py:454
  64.7 5.5 %collective-permute-start.25 = (bf16[96,256]{1,0:T(8,128)(2,1)S(1)}, bf16[96,256]{1,0:T(8,128)(2,1)S(1)}, u32[]{:S(2)}, u32[]{:S(2)}) collective-permute-start(bf16[96,256]{1,0:T(8,128)(2,1)S(1)} %add_convert_fusion.2), channel_id=1, source_target_pairs={{0,2},{1,3},{2,0},{3,1},{4,6},{5,7},{6,4},{7,5},{8,10},{9,11},{10,... | collective-permute-start | bytes 147464 | tf_op jit(solution)/shard_map/ppermute | solution.py:454
  65.7 6.0 %collective-permute-start.26 = (bf16[96,256]{1,0:T(8,128)(2,1)S(1)}, bf16[96,256]{1,0:T(8,128)(2,1)S(1)}, u32[]{:S(2)}, u32[]{:S(2)}) collective-permute-start(bf16[96,256]{1,0:T(8,128)(2,1)S(1)} %add_convert_fusion.2), channel_id=1, source_target_pairs={{0,3},{1,2},{2,1},{3,0},{4,7},{5,6},{6,5},{7,4},{8,11},{9,10},{10,... | collective-permute-start | bytes 147464 | tf_op jit(solution)/shard_map/ppermute | solution.py:454
  71.7 1.3 %collective-permute-start.27 = (bf16[96,256]{1,0:T(8,128)(2,1)S(1)}, bf16[96,256]{1,0:T(8,128)(2,1)S(1)}, u32[]{:S(2)}, u32[]{:S(2)}) collective-permute-start(bf16[96,256]{1,0:T(8,128)(2,1)S(1)} %add_convert_fusion.1.mine), channel_id=1, source_target_pairs={{0,4},{4,0},{8,12},{12,8},{16,20},{20,16},{24,28},{28,24},{1,5},{5... | collective-permute-start | bytes 147464 | tf_op jit(solution)/shard_map/ppermute | solution.py:454
where the time goes:
time: 74.5 us; the launch traced here: 74.3 us
  waiting for transfers between devices  31.4 us (42%)
  starting transfers between devices  26.2 us (35%)
  Pallas kernels  14.9 us (20%)
  between operations  1.55 us (2%)
    ppermute x28, waiting for transfers between devices, swap(): return lax.ppermute(value, axis, [(k, k ^ mask) for k in range(size)])  31.4 us
    ppermute x28, starting transfers between devices, swap(): return lax.ppermute(value, axis, [(k, k ^ mask) for k in range(size)])  26.2 us
    pallas_call x1, Pallas kernels, collect(): pl.pallas_call(functools.partial(collect_kernel, group, depth, tile_cols)...  2.44 us
    pallas_call x1, Pallas kernels, gradients(): pl.pallas_call(functools.partial(gradient_kernel, n_col, classes), out_sh...  2.44 us
    pallas_call x1, Pallas kernels, hidden_far(): pl.pallas_call(functools.partial(hidden_far_kernel, n_row, n_col), out_sh...  1.96 us
    pallas_call x1, Pallas kernels, hidden_near(): pl.pallas_call(functools.partial(hidden_near_kernel, n_row), out_shape=[j...  1.85 us
  transfers between devices with their start and end apart: 28, of which 17 were waited for; matrix products, arithmetic and copies ran while one was open for 0% of the time, Pallas kernels for 11%

commit v1 on v0

--- a/solution.py
+++ b/solution.py
@@ -131,7 +131,11 @@
     return pl.ds(pl.multiple_of(parity * (columns // 2), columns // 2), columns // 2)
 
 
-def round_kernel(n_row, total, dense):
+def first_near_kernel(n_row, ids, total, *refs):
+    pieces = refs[: n_row // 2]
+    dense, part, stacked = refs[n_row // 2 :]
+    row = ids[0]
+    stack(row, 0, pieces, stacked)
     tile_rows = dense.shape[0] // TILE
     tile_cols = dense.shape[1] // TILE
     each = tile_cols // n_row
@@ -144,40 +148,23 @@
             lanes = pl.ds(target * TILE, TILE)
             dense[lines, lanes] = total[tile_row * tile_cols + tile_col].astype(bf16)
 
-
-def round_block(total, lines, columns, n_row):
-    return pl.pallas_call(
-        functools.partial(round_kernel, n_row),
-        out_shape=jax.ShapeDtypeStruct((lines, columns), bf16),
-        in_specs=[VMEM],
-        out_specs=VMEM,
-        compiler_params=params(lines * columns * 6 + 6 * MIB),
-        cost_estimate=cost(lines * columns, lines * columns * 6),
-        name="round_block",
-    )(total)
-
-
-def first_near_kernel(n_row, ids, dense, *refs):
-    pieces = refs[: n_row // 2]
-    part, stacked = refs[n_row // 2 :]
-    row = ids[0]
-    stack(row, 0, pieces, stacked)
     part[...] = dot(dense[:, parity_columns(row & 1, dense.shape[1])], stacked[...])
 
 
-def first_near(ids, dense, pieces):
+def first_near(ids, total, pieces, n_col):
     nodes, width = pieces[0].shape
     n_row = 2 * len(pieces)
+    size = (n_col * nodes, n_row * nodes)
     return pl.pallas_call(
         functools.partial(first_near_kernel, n_row),
-        out_shape=jax.ShapeDtypeStruct((dense.shape[0], width), f32),
+        out_shape=[jax.ShapeDtypeStruct(size, bf16), jax.ShapeDtypeStruct((size[0], width), f32)],
         in_specs=[SMEM, VMEM] + [VMEM] * len(pieces),
-        out_specs=VMEM,
+        out_specs=[VMEM] * 2,
         scratch_shapes=[pltpu.VMEM((len(pieces) * nodes, width), bf16)],
-        compiler_params=params(dense.size * 2 + 6 * MIB),
-        cost_estimate=cost(dense.size * width, dense.size),
+        compiler_params=params(size[0] * size[1] * 6 + 6 * MIB),
+        cost_estimate=cost(size[0] * size[1] * width, size[0] * size[1] * 6),
         name="first_near",
-    )(ids, dense, *pieces)
+    )(ids, total, *pieces)
 
 
 def first_far_kernel(n_row, n_col, ids, dense, part, *refs):
@@ -472,6 +459,16 @@
     return value
 
 
+def sum_over_chips(value):
+    size = lax.axis_size("row")
+    masks = [1 << bit for bit in range(1, size.bit_length() - 1)]
+    for up, down in zip(masks, masks[::-1]):
+        mine = value.astype(WIRE)
+        other = lax.ppermute(mine, "row", [(k, k ^ (down if k & 1 else up)) for k in range(size)])
+        value = mine.astype(f32) + other.astype(f32)
+    return value
+
+
 def step(
     node_features,
     tile_values,
@@ -488,7 +485,7 @@
     nodes, features = node_features.shape
     classes = class_weight.shape[1]
     n_row, n_col = lax.axis_size("row"), lax.axis_size("col")
-    row_bits, col_bits = n_row.bit_length() - 1, n_col.bit_length() - 1
+    col_bits = n_col.bit_length() - 1
     lines = (classes // 16 + 1) * 16
     ids = jnp.stack([lax.axis_index("row"), lax.axis_index("col")]).astype(jnp.int32)
     code = (labels + MASK_CODE * train_mask).astype(f32)[None, :]
@@ -500,8 +497,7 @@
     total = collect(
         ids, tile_values[0, 0], tile_rows[0], tile_cols[0], tile_count, n_col * nodes // TILE, n_row * nodes // TILE
     )
-    dense = round_block(total, n_col * nodes, n_row * nodes, n_row)
-    part = first_near(ids, dense, near)
+    dense, part = first_near(ids, total, near, n_col)
     terms = first_far(ids, dense, part, far, n_col)
     arrived = [terms[0]] + [swap(terms[k], "col", k) for k in range(1, n_col)]
     first_agg = tree_sum(arrived).astype(bf16)
@@ -517,7 +513,7 @@
         ids, dense, column, slope, turned, class_turned, class_bias_lanes, class_terms, classes
     )
     part = keep.astype(f32) + swap(send, "row", 1).astype(f32)
-    part = sum_over(part, "row", 1, row_bits)
+    part = sum_over_chips(part)
     part = sum_over(part, "col", 0, col_bits)
     mine = part.astype(WIRE)
     other = swap(mine, "row", 1)

time: 74.5 us -> 74.9 us (level)
    ppermute x0 -> x2, waiting for transfers between devices: none -> 4.8 us  [sum_over_chips(): lax.ppermute(mine, 'row', [(k, k ^ (down if k & 1 else up)) for k in rang...]
    ppermute x28 -> x25, waiting for transfers between devices: 31.4 us -> 26.8 us  [swap(): return lax.ppermute(value, axis, [(k, k ^ mask) for k in range(size)])]
    ppermute x0 -> x2, starting transfers between devices: none -> 3.51 us  [sum_over_chips(): lax.ppermute(mine, 'row', [(k, k ^ (down if k & 1 else up)) for k in rang...]
    ppermute x28 -> x25, starting transfers between devices: 26.2 us -> 22.9 us  [swap(): return lax.ppermute(value, axis, [(k, k ^ mask) for k in range(size)])]
    pallas_call x2 -> x1, Pallas kernels: 2.11 us -> 2.12 us  [first_near(): pl.pallas_call(functools.partial(first_near_kernel, n_row), out_shape=[ja...]
  transfers between devices with their start and end apart: 28 -> 27, of which waited for: 17 -> 15; matrix products, arithmetic and copies ran while one was open for 0% -> 0% of each run, Pallas kernels for 11% -> 11%
where the time goes in v1:
time: 74.9 us; the launch traced here: 74.8 us
  waiting for transfers between devices  31.6 us (42%)
  starting transfers between devices  26.4 us (35%)
  Pallas kernels  14.9 us (20%)
  between operations  1.55 us (2%)
    ppermute x25, waiting for transfers between devices, swap(): return lax.ppermute(value, axis, [(k, k ^ mask) for k in range(size)])  26.8 us
    ppermute x25, starting transfers between devices, swap(): return lax.ppermute(value, axis, [(k, k ^ mask) for k in range(size)])  22.9 us
    ppermute x2, waiting for transfers between devices, sum_over_chips(): lax.ppermute(mine, 'row', [(k, k ^ (down if k & 1 else up)) for k in rang...  4.8 us
    ppermute x2, starting transfers between devices, sum_over_chips(): lax.ppermute(mine, 'row', [(k, k ^ (down if k & 1 else up)) for k in rang...  3.51 us
    pallas_call x1, Pallas kernels, gradients(): pl.pallas_call(functools.partial(gradient_kernel, n_col, classes), out_sh...  2.45 us
    pallas_call x1, Pallas kernels, collect(): pl.pallas_call(functools.partial(collect_kernel, group, depth, tile_cols)...  2.44 us
    pallas_call x1, Pallas kernels, first_near(): pl.pallas_call(functools.partial(first_near_kernel, n_row), out_shape=[ja...  2.12 us
    pallas_call x1, Pallas kernels, hidden_far(): pl.pallas_call(functools.partial(hidden_far_kernel, n_row, n_col), out_sh...  1.97 us
  transfers between devices with their start and end apart: 27, of which 15 were waited for; matrix products, arithmetic and copies ran while one was open for 0% of the time, Pallas kernels for 11%

profile of v1, /device:TPU:0, one launch (start us, length us, event | category | flops | bytes accessed | tf_op | source)
XLA Modules:
  0.0 74.8 jit_solution(2175047683216824321)
XLA Ops:
  0.6 3.0 %collective-permute-start = (bf16[256,128]{1,0:T(8,128)(2,1)}, bf16[256,128]{1,0:T(8,128)(2,1)S(1)}, u32[]{:S(2)}, u32[]{:S(2)}) collective-permute-start(bf16[256,128]{1,0:T(8,128)(2,1)} %refs_0_.1), channel_id=1, source_target_pairs={{0,8},{4,12},{8,0},{12,4},{16,24},{20,28},{24,16},{28,20},{1,9},{5... | collective-permute-start | bytes 196616 | tf_op jit(solution)/shard_map/ppermute | solution.py:441
  3.7 1.5 %collective-permute-start.1 = (bf16[256,128]{1,0:T(8,128)(2,1)}, bf16[256,128]{1,0:T(8,128)(2,1)S(1)}, u32[]{:S(2)}, u32[]{:S(2)}) collective-permute-start(bf16[256,128]{1,0:T(8,128)(2,1)} %refs_0_.1), channel_id=1, source_target_pairs={{0,16},{4,20},{8,24},{12,28},{16,0},{20,4},{24,8},{28,12},{1,17},{... | collective-permute-start | bytes 196616 | tf_op jit(solution)/shard_map/ppermute | solution.py:441
  5.2 0.0 collective-permute-start.2
  5.2 1.1 %collective-permute-done.refs_1_ = bf16[256,128]{1,0:T(8,128)(2,1)S(1)} collective-permute-done((bf16[256,128]{1,0:T(8,128)(2,1)}, bf16[256,128]{1,0:T(8,128)(2,1)S(1)}, u32[]{:S(2)}, u32[]{:S(2)}) %collective-permute-start) | collective-permute-done | bytes 65568 | tf_op jit(solution)/shard_map/ppermute | solution.py:441
  6.3 1.8 %collective-permute-done.1.refs_2_ = bf16[256,128]{1,0:T(8,128)(2,1)S(1)} collective-permute-done((bf16[256,128]{1,0:T(8,128)(2,1)}, bf16[256,128]{1,0:T(8,128)(2,1)S(1)}, u32[]{:S(2)}, u32[]{:S(2)}) %collective-permute-start.1) | collective-permute-done | bytes 65568 | tf_op jit(solution)/shard_map/ppermute | solution.py:441
  8.1 2.4 %collective-permute-done.2.refs_3_ = bf16[256,128]{1,0:T(8,128)(2,1)S(1)} collective-permute-done((bf16[256,128]{1,0:T(8,128)(2,1)}, bf16[256,128]{1,0:T(8,128)(2,1)S(1)}, u32[]{:S(2)}, u32[]{:S(2)}) %collective-permute-start.2) | collective-permute-done | bytes 65568 | tf_op jit(solution)/shard_map/ppermute | solution.py:441
  10.6 0.1 pad_add_fusion.ids
  11.3 0.0 copy-start.1
  11.3 2.4 %collect.1.total = f32[129,128,128]{2,1,0:T(8,128)S(1)} custom-call(s32[2]{0:T(128)S(1)} %pad_add_fusion.ids, s32[1,1]{1,0:T(1,128)S(6)} %copy.18.count, s32[1,384]{1,0:T(1,128)} %bitcast.20, s32[1,384]{1,0:T(1,128)} %bitcast.21, bf16[384,128,128]{2,1,0:T(8,128)(2,1)} %bitcast.18), custom_call_target="tpu_custom_call" | custom-call | flops 6291456 | bytes 12582912 | tf_op jit(solution)/shard_map/collect/pallas_call | solution.py:96
  13.8 0.0 copy-start.4
  13.8 0.0 copy-start.5
  13.8 0.0 copy-start.2
  13.8 2.1 %first_near.1 = (bf16[1024,2048]{1,0:T(8,128)(2,1)S(1)}, f32[1024,128]{1,0:T(8,128)S(1)}) custom-call(s32[2]{0:T(128)S(1)} %pad_add_fusion.ids, f32[129,128,128]{2,1,0:T(8,128)S(1)} %collect.1.total, bf16[256,128]{1,0:T(8,128)(2,1)S(1)} %copy-done.1, bf16[256,128]{1,0:T(8,128)(2,1)S(1)} %collective-permute-done.refs_1_, ...), custom_call_target="tpu_custom_call" | custom-call | flops 268435456 | bytes 12582912 | tf_op jit(solution)/shard_map/first_near/pallas_call | solution.py:158
  16.0 1.3 %first_far.1 = (bf16[256,128]{1,0:T(8,128)(2,1)S(1)}, bf16[256,128]{1,0:T(8,128)(2,1)S(1)}, bf16[256,128]{1,0:T(8,128)(2,1)S(1)}, bf16[256,128]{1,0:T(8,128)(2,1)S(1)}) custom-call(s32[2]{0:T(128)S(1)} %pad_add_fusion.ids, bf16[1024,2048]{1,0:T(8,128)(2,1)S(1)} %get-tuple-element.28.dense, f32[1024,128]{1,0:T(8,128)S(1)} %get-tuple-element.29.part, ...), custom_call_target="tpu_custom_call" | custom-call | flops 268435456 | bytes 2097152 | tf_op jit(solution)/shard_map/first_far/pallas_call | solution.py:185
  17.3 1.6 %collective-permute-start.7 = (bf16[256,128]{1,0:T(8,128)(2,1)S(1)}, bf16[256,128]{1,0:T(8,128)(2,1)S(1)}, u32[]{:S(2)}, u32[]{:S(2)}) collective-permute-start(bf16[256,128]{1,0:T(8,128)(2,1)S(1)} %get-tuple-element.31), channel_id=1, source_target_pairs={{0,1},{1,0},{2,3},{3,2},{4,5},{5,4},{6,7},{7,6},{8,9},{9,8},{10,11... | collective-permute-start | bytes 196616 | tf_op jit(solution)/shard_map/ppermute | solution.py:441
  18.9 3.2 %collective-permute-start.8 = (bf16[256,128]{1,0:T(8,128)(2,1)S(1)}, bf16[256,128]{1,0:T(8,128)(2,1)S(1)}, u32[]{:S(2)}, u32[]{:S(2)}) collective-permute-start(bf16[256,128]{1,0:T(8,128)(2,1)S(1)} %get-tuple-element.32), channel_id=1, source_target_pairs={{0,2},{1,3},{2,0},{3,1},{4,6},{5,7},{6,4},{7,5},{8,10},{9,11},{10,... | collective-permute-start | bytes 196616 | tf_op jit(solution)/shard_map/ppermute | solution.py:441
  22.1 0.0 collective-permute-start.9
  22.2 4.3 %collective-permute-done.8 = bf16[256,128]{1,0:T(8,128)(2,1)S(1)} collective-permute-done((bf16[256,128]{1,0:T(8,128)(2,1)S(1)}, bf16[256,128]{1,0:T(8,128)(2,1)S(1)}, u32[]{:S(2)}, u32[]{:S(2)}) %collective-permute-start.8) | collective-permute-done | bytes 65568 | tf_op jit(solution)/shard_map/ppermute | solution.py:441
  26.5 1.8 %collective-permute-done.9 = bf16[256,128]{1,0:T(8,128)(2,1)S(1)} collective-permute-done((bf16[256,128]{1,0:T(8,128)(2,1)S(1)}, bf16[256,128]{1,0:T(8,128)(2,1)S(1)}, u32[]{:S(2)}, u32[]{:S(2)}) %collective-permute-start.9) | collective-permute-done | bytes 65568 | tf_op jit(solution)/shard_map/ppermute | solution.py:441
  28.3 0.9 %collective-permute-start.10 = (bf16[256,128]{1,0:T(8,128)(2,1)S(1)}, bf16[256,128]{1,0:T(8,128)(2,1)S(1)}, u32[]{:S(2)}, u32[]{:S(2)}) collective-permute-start(bf16[256,128]{1,0:T(8,128)(2,1)S(1)} %add_convert_fusion.refs_0_), channel_id=1, source_target_pairs={{0,8},{4,12},{8,0},{12,4},{16,24},{20,28},{24,16},{28,20},{1,9},{5... | collective-permute-start | bytes 196616 | tf_op jit(solution)/shard_map/ppermute | solution.py:441
  29.2 0.4 collective-permute-start.11
  29.6 2.3 %collective-permute-start.12 = (bf16[256,128]{1,0:T(8,128)(2,1)S(1)}, bf16[256,128]{1,0:T(8,128)(2,1)S(1)}, u32[]{:S(2)}, u32[]{:S(2)}) collective-permute-start(bf16[256,128]{1,0:T(8,128)(2,1)S(1)} %add_convert_fusion.refs_0_), channel_id=1, source_target_pairs={{0,24},{4,28},{8,16},{12,20},{16,8},{20,12},{24,0},{28,4},{1,25},{... | collective-permute-start | bytes 196616 | tf_op jit(solution)/shard_map/ppermute | solution.py:441
  31.9 1.3 %collective-permute-done.10.refs_1_.refs_2_ = bf16[256,128]{1,0:T(8,128)(2,1)S(1)} collective-permute-done((bf16[256,128]{1,0:T(8,128)(2,1)S(1)}, bf16[256,128]{1,0:T(8,128)(2,1)S(1)}, u32[]{:S(2)}, u32[]{:S(2)}) %collective-permute-start.10) | collective-permute-done | bytes 65568 | tf_op jit(solution)/shard_map/ppermute | solution.py:441
  33.2 1.7 %collective-permute-done.11.refs_2_.refs_4_ = bf16[256,128]{1,0:T(8,128)(2,1)S(1)} collective-permute-done((bf16[256,128]{1,0:T(8,128)(2,1)S(1)}, bf16[256,128]{1,0:T(8,128)(2,1)S(1)}, u32[]{:S(2)}, u32[]{:S(2)}) %collective-permute-start.11) | collective-permute-done | bytes 65568 | tf_op jit(solution)/shard_map/ppermute | solution.py:441
  34.9 0.5 collective-permute-start.16
  35.5 1.9 %hidden_near.1 = (bf16[256,256]{1,0:T(8,128)(2,1)}, bf16[1024,256]{1,0:T(8,128)(2,1)S(1)}, f32[1024,128]{1,0:T(8,128)S(1)}) custom-call(s32[2]{0:T(128)S(1)} %pad_add_fusion.ids, bf16[1024,2048]{1,0:T(8,128)(2,1)S(1)} %get-tuple-element.28.dense, bf16[128,256]{1,0:T(8,128)(2,1)S(1)} %copy-done, f32[1,256]{1,0:T(1,128)S(1)} %bitcast.15, ...), custom_call_target="tpu_custom_call" | custom-call | flops 536870912 | bytes 2097152 | tf_op jit(solution)/shard_map/hidden_near/pallas_call | solution.py:230
  37.4 2.0 %hidden_far.1 = (bf16[2048,256]{1,0:T(8,128)(2,1)S(1)}, bf16[48,1024]{1,0:T(8,128)(2,1)S(1)}) custom-call(s32[2]{0:T(128)S(1)} %pad_add_fusion.ids, bf16[1024,2048]{1,0:T(8,128)(2,1)S(1)} %get-tuple-element.28.dense, bf16[128,256]{1,0:T(8,128)(2,1)S(1)} %copy-done, f32[1,256]{1,0:T(1,128)S(1)} %bitcast.16, ...), custom_call_target="tpu_custom_call" | custom-call | flops 536870912 | bytes 2097152 | tf_op jit(solution)/shard_map/hidden_far/pallas_call | solution.py:268
  39.3 0.6 collective-permute-start.17
  39.9 1.9 %collective-permute-start.18 = (bf16[48,1024]{1,0:T(8,128)(2,1)S(1)}, bf16[48,1024]{1,0:T(8,128)(2,1)S(1)}, u32[]{:S(2)}, u32[]{:S(2)}) collective-permute-start(bf16[48,1024]{1,0:T(8,128)(2,1)S(1)} %get-tuple-element.40.refs_0_), channel_id=1, source_target_pairs={{0,2},{1,3},{2,0},{3,1},{4,6},{5,7},{6,4},{7,5},{8,10},{9,11},{10,... | collective-permute-start | bytes 294920 | tf_op jit(solution)/shard_map/ppermute | solution.py:441
  41.8 2.0 %collective-permute-start.19 = (bf16[48,1024]{1,0:T(8,128)(2,1)S(1)}, bf16[48,1024]{1,0:T(8,128)(2,1)S(1)}, u32[]{:S(2)}, u32[]{:S(2)}) collective-permute-start(bf16[48,1024]{1,0:T(8,128)(2,1)S(1)} %get-tuple-element.40.refs_0_), channel_id=1, source_target_pairs={{0,3},{1,2},{2,1},{3,0},{4,7},{5,6},{6,5},{7,4},{8,11},{9,10},{10,... | collective-permute-start | bytes 294920 | tf_op jit(solution)/shard_map/ppermute | solution.py:441
  43.8 1.5 %slopes.1 = (f32[2048,256]{1,0:T(8,128)S(1)}, bf16[128,2048]{1,0:T(8,128)(2,1)S(1)}) custom-call(s32[2]{0:T(128)S(1)} %pad_add_fusion.ids, bf16[128,256]{1,0:T(8,128)(2,1)S(1)} %copy-done, f32[1,256]{1,0:T(1,128)S(1)} %bitcast.17, bf16[256,128]{1,0:T(8,128)(2,1)S(1)} %add_convert_fusion.refs_0_, ...), custom_call_target="tpu_custom_call" | custom-call | flops 134217728 | bytes 2097152 | tf_op jit(solution)/shard_map/slopes/pallas_call | solution.py:301
  45.3 0.5 collective-permute-done.17.refs_1_
  45.8 4.8 %collective-permute-done.18.refs_2_ = bf16[48,1024]{1,0:T(8,128)(2,1)S(1)} collective-permute-done((bf16[48,1024]{1,0:T(8,128)(2,1)S(1)}, bf16[48,1024]{1,0:T(8,128)(2,1)S(1)}, u32[]{:S(2)}, u32[]{:S(2)}) %collective-permute-start.18) | collective-permute-done | bytes 98336 | tf_op jit(solution)/shard_map/ppermute | solution.py:441
  50.6 2.5 %gradients.1 = (f32[47,256]{1,0:T(8,128)}, bf16[96,256]{1,0:T(8,128)(2,1)S(1)}, bf16[96,256]{1,0:T(8,128)(2,1)S(1)}) custom-call(s32[2]{0:T(128)S(1)} %pad_add_fusion.ids, bf16[1024,2048]{1,0:T(8,128)(2,1)S(1)} %get-tuple-element.28.dense, bf16[2048,256]{1,0:T(8,128)(2,1)S(1)} %get-tuple-element.37.column, f32[2048,256]{1,0:T(8,128)S(1)} %get-tuple-element.38.slope, ...), custom_call_target="tpu_custom_call" | custom-call | flops 402653184 | bytes 4194304 | tf_op jit(solution)/shard_map/gradients/pallas_call | solution.py:386
  53.1 0.1 collective-permute-start.20
  53.1 1.2 %collective-permute-done.20 = bf16[96,256]{1,0:T(8,128)(2,1)S(1)} collective-permute-done((bf16[96,256]{1,0:T(8,128)(2,1)S(1)}, bf16[96,256]{1,0:T(8,128)(2,1)S(1)}, u32[]{:S(2)}, u32[]{:S(2)}) %collective-permute-start.20) | collective-permute-done | bytes 49184 | tf_op jit(solution)/shard_map/ppermute | solution.py:441
  54.4 2.1 %collective-permute-start.21 = (bf16[96,256]{1,0:T(8,128)(2,1)S(1)}, bf16[96,256]{1,0:T(8,128)(2,1)S(1)}, u32[]{:S(2)}, u32[]{:S(2)}) collective-permute-start(bf16[96,256]{1,0:T(8,128)(2,1)S(1)} %add_convert_fusion.4), channel_id=1, source_target_pairs={{0,8},{4,20},{8,0},{12,28},{16,24},{20,4},{24,16},{28,12},{1,9},{5... | collective-permute-start | bytes 147464 | tf_op jit(solution)/shard_map/ppermute | solution.py:467
  56.5 2.1 %collective-permute-done.21 = bf16[96,256]{1,0:T(8,128)(2,1)S(1)} collective-permute-done((bf16[96,256]{1,0:T(8,128)(2,1)S(1)}, bf16[96,256]{1,0:T(8,128)(2,1)S(1)}, u32[]{:S(2)}, u32[]{:S(2)}) %collective-permute-start.21) | collective-permute-done | bytes 49184 | tf_op jit(solution)/shard_map/ppermute | solution.py:467
  58.5 1.4 %collective-permute-start.22 = (bf16[96,256]{1,0:T(8,128)(2,1)S(1)}, bf16[96,256]{1,0:T(8,128)(2,1)S(1)}, u32[]{:S(2)}, u32[]{:S(2)}) collective-permute-start(bf16[96,256]{1,0:T(8,128)(2,1)S(1)} %add_convert_fusion.3), channel_id=1, source_target_pairs={{0,16},{4,12},{8,24},{12,4},{16,0},{20,28},{24,8},{28,20},{1,17},{... | collective-permute-start | bytes 147464 | tf_op jit(solution)/shard_map/ppermute | solution.py:467
  60.0 2.7 %collective-permute-done.22 = bf16[96,256]{1,0:T(8,128)(2,1)S(1)} collective-permute-done((bf16[96,256]{1,0:T(8,128)(2,1)S(1)}, bf16[96,256]{1,0:T(8,128)(2,1)S(1)}, u32[]{:S(2)}, u32[]{:S(2)}) %collective-permute-start.22) | collective-permute-done | bytes 49184 | tf_op jit(solution)/shard_map/ppermute | solution.py:467
  62.7 2.1 %collective-permute-start.23 = (bf16[96,256]{1,0:T(8,128)(2,1)S(1)}, bf16[96,256]{1,0:T(8,128)(2,1)S(1)}, u32[]{:S(2)}, u32[]{:S(2)}) collective-permute-start(bf16[96,256]{1,0:T(8,128)(2,1)S(1)} %add_convert_fusion.2), channel_id=1, source_target_pairs={{0,1},{1,0},{2,3},{3,2},{4,5},{5,4},{6,7},{7,6},{8,9},{9,8},{10,11... | collective-permute-start | bytes 147464 | tf_op jit(solution)/shard_map/ppermute | solution.py:441
  64.8 1.3 %collective-permute-start.24 = (bf16[96,256]{1,0:T(8,128)(2,1)S(1)}, bf16[96,256]{1,0:T(8,128)(2,1)S(1)}, u32[]{:S(2)}, u32[]{:S(2)}) collective-permute-start(bf16[96,256]{1,0:T(8,128)(2,1)S(1)} %add_convert_fusion.2), channel_id=1, source_target_pairs={{0,2},{1,3},{2,0},{3,1},{4,6},{5,7},{6,4},{7,5},{8,10},{9,11},{10,... | collective-permute-start | bytes 147464 | tf_op jit(solution)/shard_map/ppermute | solution.py:441
  66.1 1.4 %collective-permute-start.25 = (bf16[96,256]{1,0:T(8,128)(2,1)S(1)}, bf16[96,256]{1,0:T(8,128)(2,1)S(1)}, u32[]{:S(2)}, u32[]{:S(2)}) collective-permute-start(bf16[96,256]{1,0:T(8,128)(2,1)S(1)} %add_convert_fusion.2), channel_id=1, source_target_pairs={{0,3},{1,2},{2,1},{3,0},{4,7},{5,6},{6,5},{7,4},{8,11},{9,10},{10,... | collective-permute-start | bytes 147464 | tf_op jit(solution)/shard_map/ppermute | solution.py:441
  67.5 2.8 %collective-permute-done.24 = bf16[96,256]{1,0:T(8,128)(2,1)S(1)} collective-permute-done((bf16[96,256]{1,0:T(8,128)(2,1)S(1)}, bf16[96,256]{1,0:T(8,128)(2,1)S(1)}, u32[]{:S(2)}, u32[]{:S(2)}) %collective-permute-start.24) | collective-permute-done | bytes 49184 | tf_op jit(solution)/shard_map/ppermute | solution.py:441
  70.4 1.8 %collective-permute-done.25 = bf16[96,256]{1,0:T(8,128)(2,1)S(1)} collective-permute-done((bf16[96,256]{1,0:T(8,128)(2,1)S(1)}, bf16[96,256]{1,0:T(8,128)(2,1)S(1)}, u32[]{:S(2)}, u32[]{:S(2)}) %collective-permute-start.25) | collective-permute-done | bytes 49184 | tf_op jit(solution)/shard_map/ppermute | solution.py:441
  72.2 0.1 collective-permute-start.26
  72.2 1.2 %collective-permute-done.26.other = bf16[96,256]{1,0:T(8,128)(2,1)S(1)} collective-permute-done((bf16[96,256]{1,0:T(8,128)(2,1)S(1)}, bf16[96,256]{1,0:T(8,128)(2,1)S(1)}, u32[]{:S(2)}, u32[]{:S(2)}) %collective-permute-start.26) | collective-permute-done | bytes 49184 | tf_op jit(solution)/shard_map/ppermute | solution.py:441
  73.4 1.3 %finish.1 = (f32[1,1]{1,0:T(1,128)}, f32[128,256]{1,0:T(8,128)}, f32[1,256]{1,0:T(1,128)}, f32[47,256]{1,0:T(8,128)}, f32[1,47]{1,0:T(1,128)}) custom-call(s32[2]{0:T(128)S(1)} %pad_add_fusion.ids, bf16[96,256]{1,0:T(8,128)(2,1)S(1)} %add_convert_fusion.1.mine, bf16[96,256]{1,0:T(8,128)(2,1)S(1)} %collective-permute-done.26.other), custom_call_target="tpu_custom_call" | custom-call | tf_op jit(solution)/shard_map/finish/pallas_call | solution.py:422
  (37 shorter events, 0.2 us)
Async XLA Ops:
  0.6 5.7 %collective-permute-start = (bf16[256,128]{1,0:T(8,128)(2,1)}, bf16[256,128]{1,0:T(8,128)(2,1)S(1)}, u32[]{:S(2)}, u32[]{:S(2)}) collective-permute-start(bf16[256,128]{1,0:T(8,128)(2,1)} %refs_0_.1), channel_id=1, source_target_pairs={{0,8},{4,12},{8,0},{12,4},{16,24},{20,28},{24,16},{28,20},{1,9},{5... | collective-permute-start | bytes 196616 | tf_op jit(solution)/shard_map/ppermute | solution.py:441
  3.7 4.5 %collective-permute-start.1 = (bf16[256,128]{1,0:T(8,128)(2,1)}, bf16[256,128]{1,0:T(8,128)(2,1)S(1)}, u32[]{:S(2)}, u32[]{:S(2)}) collective-permute-start(bf16[256,128]{1,0:T(8,128)(2,1)} %refs_0_.1), channel_id=1, source_target_pairs={{0,16},{4,20},{8,24},{12,28},{16,0},{20,4},{24,8},{28,12},{1,17},{... | collective-permute-start | bytes 196616 | tf_op jit(solution)/shard_map/ppermute | solution.py:441
  5.2 5.4 %collective-permute-start.2 = (bf16[256,128]{1,0:T(8,128)(2,1)}, bf16[256,128]{1,0:T(8,128)(2,1)S(1)}, u32[]{:S(2)}, u32[]{:S(2)}) collective-permute-start(bf16[256,128]{1,0:T(8,128)(2,1)} %refs_0_.1), channel_id=1, source_target_pairs={{0,24},{4,28},{8,16},{12,20},{16,8},{20,12},{24,0},{28,4},{1,25},{... | collective-permute-start | bytes 196616 | tf_op jit(solution)/shard_map/ppermute | solution.py:441
  5.2 10.8 %collective-permute-start.3 = (bf16[256,128]{1,0:T(8,128)(2,1)}, bf16[256,128]{1,0:T(8,128)(2,1)S(1)}, u32[]{:S(2)}, u32[]{:S(2)}) collective-permute-start(bf16[256,128]{1,0:T(8,128)(2,1)} %refs_0_.1), channel_id=1, source_target_pairs={{0,4},{4,0},{8,12},{12,8},{16,20},{20,16},{24,28},{28,24},{1,5},{5... | collective-permute-start | bytes 196616 | tf_op jit(solution)/shard_map/ppermute | solution.py:441
  6.3 9.6 %collective-permute-start.4 = (bf16[256,128]{1,0:T(8,128)(2,1)S(1)}, bf16[256,128]{1,0:T(8,128)(2,1)S(1)}, u32[]{:S(2)}, u32[]{:S(2)}) collective-permute-start(bf16[256,128]{1,0:T(8,128)(2,1)S(1)} %collective-permute-done.refs_1_), channel_id=1, source_target_pairs={{0,4},{4,0},{8,12},{12,8},{16,20},{20,16},{24,28},{28,24},{1,5},{5... | collective-permute-start | bytes 196616 | tf_op jit(solution)/shard_map/ppermute | solution.py:441
  8.1 7.8 %collective-permute-start.5 = (bf16[256,128]{1,0:T(8,128)(2,1)S(1)}, bf16[256,128]{1,0:T(8,128)(2,1)S(1)}, u32[]{:S(2)}, u32[]{:S(2)}) collective-permute-start(bf16[256,128]{1,0:T(8,128)(2,1)S(1)} %collective-permute-done.1.refs_2_), channel_id=1, source_target_pairs={{0,4},{4,0},{8,12},{12,8},{16,20},{20,16},{24,28},{28,24},{1,5},{5... | collective-permute-start | bytes 196616 | tf_op jit(solution)/shard_map/ppermute | solution.py:441
  10.6 5.4 %collective-permute-start.6 = (bf16[256,128]{1,0:T(8,128)(2,1)S(1)}, bf16[256,128]{1,0:T(8,128)(2,1)S(1)}, u32[]{:S(2)}, u32[]{:S(2)}) collective-permute-start(bf16[256,128]{1,0:T(8,128)(2,1)S(1)} %collective-permute-done.2.refs_3_), channel_id=1, source_target_pairs={{0,4},{4,0},{8,12},{12,8},{16,20},{20,16},{24,28},{28,24},{1,5},{5... | collective-permute-start | bytes 196616 | tf_op jit(solution)/shard_map/ppermute | solution.py:441
  11.3 2.5 %copy-start.1 = (bf16[256,128]{1,0:T(8,128)(2,1)S(1)}, bf16[256,128]{1,0:T(8,128)(2,1)}, u32[]{:S(2)}) copy-start(bf16[256,128]{1,0:T(8,128)(2,1)} %refs_0_.1) | copy-start | bytes 196612
  13.8 21.6 %copy-start.4 = (s32[256]{0:T(256)S(1)}, s32[256]{0:T(256)}, u32[]{:S(2)}) copy-start(s32[256]{0:T(256)} %param.16) | copy-start | bytes 3076
  13.8 21.6 %copy-start.5 = (s32[256]{0:T(256)S(1)}, s32[256]{0:T(256)}, u32[]{:S(2)}) copy-start(s32[256]{0:T(256)} %param.17) | copy-start | bytes 3076
  13.8 21.6 %copy-start.3 = (bf16[256,47]{0,1:T(8,128)(2,1)S(1)}, bf16[256,47]{0,1:T(8,128)(2,1)}, u32[]{:S(2)}) copy-start(bf16[256,47]{0,1:T(8,128)(2,1)} %param.20) | copy-start | bytes 72196
  13.8 21.6 %copy-start = (bf16[128,256]{1,0:T(8,128)(2,1)S(1)}, bf16[128,256]{1,0:T(8,128)(2,1)}, u32[]{:S(2)}) copy-start(bf16[128,256]{1,0:T(8,128)(2,1)} %weight.5) | copy-start | bytes 196612
  13.8 21.6 %copy-start.2 = (f32[256]{0:T(256)S(1)}, f32[256]{0:T(256)}, u32[]{:S(2)}) copy-start(f32[256]{0:T(256)} %param.19) | copy-start | bytes 3076
  15.9 27.8 %copy-start.6 = (f32[47]{0:T(128)S(1)}, f32[47]{0:T(128)}, u32[]{:S(2)}) copy-start(f32[47]{0:T(128)} %param.21) | copy-start | bytes 568
  17.3 4.9 %collective-permute-start.7 = (bf16[256,128]{1,0:T(8,128)(2,1)S(1)}, bf16[256,128]{1,0:T(8,128)(2,1)S(1)}, u32[]{:S(2)}, u32[]{:S(2)}) collective-permute-start(bf16[256,128]{1,0:T(8,128)(2,1)S(1)} %get-tuple-element.31), channel_id=1, source_target_pairs={{0,1},{1,0},{2,3},{3,2},{4,5},{5,4},{6,7},{7,6},{8,9},{9,8},{10,11... | collective-permute-start | bytes 196616 | tf_op jit(solution)/shard_map/ppermute | solution.py:441
  18.9 7.6 %collective-permute-start.8 = (bf16[256,128]{1,0:T(8,128)(2,1)S(1)}, bf16[256,128]{1,0:T(8,128)(2,1)S(1)}, u32[]{:S(2)}, u32[]{:S(2)}) collective-permute-start(bf16[256,128]{1,0:T(8,128)(2,1)S(1)} %get-tuple-element.32), channel_id=1, source_target_pairs={{0,2},{1,3},{2,0},{3,1},{4,6},{5,7},{6,4},{7,5},{8,10},{9,11},{10,... | collective-permute-start | bytes 196616 | tf_op jit(solution)/shard_map/ppermute | solution.py:441
  22.1 6.2 %collective-permute-start.9 = (bf16[256,128]{1,0:T(8,128)(2,1)S(1)}, bf16[256,128]{1,0:T(8,128)(2,1)S(1)}, u32[]{:S(2)}, u32[]{:S(2)}) collective-permute-start(bf16[256,128]{1,0:T(8,128)(2,1)S(1)} %get-tuple-element.33), channel_id=1, source_target_pairs={{0,3},{1,2},{2,1},{3,0},{4,7},{5,6},{6,5},{7,4},{8,11},{9,10},{10,... | collective-permute-start | bytes 196616 | tf_op jit(solution)/shard_map/ppermute | solution.py:441
  28.3 4.9 %collective-permute-start.10 = (bf16[256,128]{1,0:T(8,128)(2,1)S(1)}, bf16[256,128]{1,0:T(8,128)(2,1)S(1)}, u32[]{:S(2)}, u32[]{:S(2)}) collective-permute-start(bf16[256,128]{1,0:T(8,128)(2,1)S(1)} %add_convert_fusion.refs_0_), channel_id=1, source_target_pairs={{0,8},{4,12},{8,0},{12,4},{16,24},{20,28},{24,16},{28,20},{1,9},{5... | collective-permute-start | bytes 196616 | tf_op jit(solution)/shard_map/ppermute | solution.py:441
  29.2 5.7 %collective-permute-start.11 = (bf16[256,128]{1,0:T(8,128)(2,1)S(1)}, bf16[256,128]{1,0:T(8,128)(2,1)S(1)}, u32[]{:S(2)}, u32[]{:S(2)}) collective-permute-start(bf16[256,128]{1,0:T(8,128)(2,1)S(1)} %add_convert_fusion.refs_0_), channel_id=1, source_target_pairs={{0,16},{4,20},{8,24},{12,28},{16,0},{20,4},{24,8},{28,12},{1,17},{... | collective-permute-start | bytes 196616 | tf_op jit(solution)/shard_map/ppermute | solution.py:441
  29.6 5.3 %collective-permute-start.12 = (bf16[256,128]{1,0:T(8,128)(2,1)S(1)}, bf16[256,128]{1,0:T(8,128)(2,1)S(1)}, u32[]{:S(2)}, u32[]{:S(2)}) collective-permute-start(bf16[256,128]{1,0:T(8,128)(2,1)S(1)} %add_convert_fusion.refs_0_), channel_id=1, source_target_pairs={{0,24},{4,28},{8,16},{12,20},{16,8},{20,12},{24,0},{28,4},{1,25},{... | collective-permute-start | bytes 196616 | tf_op jit(solution)/shard_map/ppermute | solution.py:441
  31.9 5.4 %collective-permute-start.13 = (bf16[256,128]{1,0:T(8,128)(2,1)S(1)}, bf16[256,128]{1,0:T(8,128)(2,1)S(1)}, u32[]{:S(2)}, u32[]{:S(2)}) collective-permute-start(bf16[256,128]{1,0:T(8,128)(2,1)S(1)} %add_convert_fusion.refs_0_), channel_id=1, source_target_pairs={{0,4},{4,0},{8,12},{12,8},{16,20},{20,16},{24,28},{28,24},{1,5},{5... | collective-permute-start | bytes 196616 | tf_op jit(solution)/shard_map/ppermute | solution.py:441
  33.2 4.1 %collective-permute-start.14 = (bf16[256,128]{1,0:T(8,128)(2,1)S(1)}, bf16[256,128]{1,0:T(8,128)(2,1)S(1)}, u32[]{:S(2)}, u32[]{:S(2)}) collective-permute-start(bf16[256,128]{1,0:T(8,128)(2,1)S(1)} %collective-permute-done.10.refs_1_.refs_2_), channel_id=1, source_target_pairs={{0,4},{4,0},{8,12},{12,8},{16,20},{20,16},{24,28},{28,24},{1,5},{5... | collective-permute-start | bytes 196616 | tf_op jit(solution)/shard_map/ppermute | solution.py:441
  34.9 2.5 %collective-permute-start.15 = (bf16[256,128]{1,0:T(8,128)(2,1)S(1)}, bf16[256,128]{1,0:T(8,128)(2,1)S(1)}, u32[]{:S(2)}, u32[]{:S(2)}) collective-permute-start(bf16[256,128]{1,0:T(8,128)(2,1)S(1)} %collective-permute-done.11.refs_2_.refs_4_), channel_id=1, source_target_pairs={{0,4},{4,0},{8,12},{12,8},{16,20},{20,16},{24,28},{28,24},{1,5},{5... | collective-permute-start | bytes 196616 | tf_op jit(solution)/shard_map/ppermute | solution.py:441
  34.9 2.5 %collective-permute-start.16 = (bf16[256,128]{1,0:T(8,128)(2,1)S(1)}, bf16[256,128]{1,0:T(8,128)(2,1)S(1)}, u32[]{:S(2)}, u32[]{:S(2)}) collective-permute-start(bf16[256,128]{1,0:T(8,128)(2,1)S(1)} %collective-permute-done.12.refs_3_.refs_6_), channel_id=1, source_target_pairs={{0,4},{4,0},{8,12},{12,8},{16,20},{20,16},{24,28},{28,24},{1,5},{5... | collective-permute-start | bytes 196616 | tf_op jit(solution)/shard_map/ppermute | solution.py:441
  39.3 6.5 %collective-permute-start.17 = (bf16[48,1024]{1,0:T(8,128)(2,1)S(1)}, bf16[48,1024]{1,0:T(8,128)(2,1)S(1)}, u32[]{:S(2)}, u32[]{:S(2)}) collective-permute-start(bf16[48,1024]{1,0:T(8,128)(2,1)S(1)} %get-tuple-element.40.refs_0_), channel_id=1, source_target_pairs={{0,1},{1,0},{2,3},{3,2},{4,5},{5,4},{6,7},{7,6},{8,9},{9,8},{10,11... | collective-permute-start | bytes 294920 | tf_op jit(solution)/shard_map/ppermute | solution.py:441
  39.9 10.7 %collective-permute-start.18 = (bf16[48,1024]{1,0:T(8,128)(2,1)S(1)}, bf16[48,1024]{1,0:T(8,128)(2,1)S(1)}, u32[]{:S(2)}, u32[]{:S(2)}) collective-permute-start(bf16[48,1024]{1,0:T(8,128)(2,1)S(1)} %get-tuple-element.40.refs_0_), channel_id=1, source_target_pairs={{0,2},{1,3},{2,0},{3,1},{4,6},{5,7},{6,4},{7,5},{8,10},{9,11},{10,... | collective-permute-start | bytes 294920 | tf_op jit(solution)/shard_map/ppermute | solution.py:441
  41.8 8.8 %collective-permute-start.19 = (bf16[48,1024]{1,0:T(8,128)(2,1)S(1)}, bf16[48,1024]{1,0:T(8,128)(2,1)S(1)}, u32[]{:S(2)}, u32[]{:S(2)}) collective-permute-start(bf16[48,1024]{1,0:T(8,128)(2,1)S(1)} %get-tuple-element.40.refs_0_), channel_id=1, source_target_pairs={{0,3},{1,2},{2,1},{3,0},{4,7},{5,6},{6,5},{7,4},{8,11},{9,10},{10,... | collective-permute-start | bytes 294920 | tf_op jit(solution)/shard_map/ppermute | solution.py:441
  53.1 1.3 %collective-permute-start.20 = (bf16[96,256]{1,0:T(8,128)(2,1)S(1)}, bf16[96,256]{1,0:T(8,128)(2,1)S(1)}, u32[]{:S(2)}, u32[]{:S(2)}) collective-permute-start(bf16[96,256]{1,0:T(8,128)(2,1)S(1)} %get-tuple-element.43), channel_id=1, source_target_pairs={{0,4},{4,0},{8,12},{12,8},{16,20},{20,16},{24,28},{28,24},{1,5},{5... | collective-permute-start | bytes 147464 | tf_op jit(solution)/shard_map/ppermute | solution.py:441
  54.4 4.2 %collective-permute-start.21 = (bf16[96,256]{1,0:T(8,128)(2,1)S(1)}, bf16[96,256]{1,0:T(8,128)(2,1)S(1)}, u32[]{:S(2)}, u32[]{:S(2)}) collective-permute-start(bf16[96,256]{1,0:T(8,128)(2,1)S(1)} %add_convert_fusion.4), channel_id=1, source_target_pairs={{0,8},{4,20},{8,0},{12,28},{16,24},{20,4},{24,16},{28,12},{1,9},{5... | collective-permute-start | bytes 147464 | tf_op jit(solution)/shard_map/ppermute | solution.py:467
  58.5 4.2 %collective-permute-start.22 = (bf16[96,256]{1,0:T(8,128)(2,1)S(1)}, bf16[96,256]{1,0:T(8,128)(2,1)S(1)}, u32[]{:S(2)}, u32[]{:S(2)}) collective-permute-start(bf16[96,256]{1,0:T(8,128)(2,1)S(1)} %add_convert_fusion.3), channel_id=1, source_target_pairs={{0,16},{4,12},{8,24},{12,4},{16,0},{20,28},{24,8},{28,20},{1,17},{... | collective-permute-start | bytes 147464 | tf_op jit(solution)/shard_map/ppermute | solution.py:467
  62.7 4.8 %collective-permute-start.23 = (bf16[96,256]{1,0:T(8,128)(2,1)S(1)}, bf16[96,256]{1,0:T(8,128)(2,1)S(1)}, u32[]{:S(2)}, u32[]{:S(2)}) collective-permute-start(bf16[96,256]{1,0:T(8,128)(2,1)S(1)} %add_convert_fusion.2), channel_id=1, source_target_pairs={{0,1},{1,0},{2,3},{3,2},{4,5},{5,4},{6,7},{7,6},{8,9},{9,8},{10,11... | collective-permute-start | bytes 147464 | tf_op jit(solution)/shard_map/ppermute | solution.py:441
  64.8 5.5 %collective-permute-start.24 = (bf16[96,256]{1,0:T(8,128)(2,1)S(1)}, bf16[96,256]{1,0:T(8,128)(2,1)S(1)}, u32[]{:S(2)}, u32[]{:S(2)}) collective-permute-start(bf16[96,256]{1,0:T(8,128)(2,1)S(1)} %add_convert_fusion.2), channel_id=1, source_target_pairs={{0,2},{1,3},{2,0},{3,1},{4,6},{5,7},{6,4},{7,5},{8,10},{9,11},{10,... | collective-permute-start | bytes 147464 | tf_op jit(solution)/shard_map/ppermute | solution.py:441
  66.1 6.0 %collective-permute-start.25 = (bf16[96,256]{1,0:T(8,128)(2,1)S(1)}, bf16[96,256]{1,0:T(8,128)(2,1)S(1)}, u32[]{:S(2)}, u32[]{:S(2)}) collective-permute-start(bf16[96,256]{1,0:T(8,128)(2,1)S(1)} %add_convert_fusion.2), channel_id=1, source_target_pairs={{0,3},{1,2},{2,1},{3,0},{4,7},{5,6},{6,5},{7,4},{8,11},{9,10},{10,... | collective-permute-start | bytes 147464 | tf_op jit(solution)/shard_map/ppermute | solution.py:441
  72.2 1.3 %collective-permute-start.26 = (bf16[96,256]{1,0:T(8,128)(2,1)S(1)}, bf16[96,256]{1,0:T(8,128)(2,1)S(1)}, u32[]{:S(2)}, u32[]{:S(2)}) collective-permute-start(bf16[96,256]{1,0:T(8,128)(2,1)S(1)} %add_convert_fusion.1.mine), channel_id=1, source_target_pairs={{0,4},{4,0},{8,12},{12,8},{16,20},{20,16},{24,28},{28,24},{1,5},{5... | collective-permute-start | bytes 147464 | tf_op jit(solution)/shard_map/ppermute | solution.py:441
